TPU v7x, 256 devices: a whole 4x4x8 slice. The times are simulated.
256 devices in a mesh: ctx: 32 (over x, z), head: 8 (over y, core).
Axes of the slice: x: 4, y: 4, z: 8, core: 2. Of those that a mesh axis runs over, the one named last changes fastest.
Arguments:
- query_vectors: bfloat16 [12288, 4096], P('ctx', 'head'), may hold values from -6 to 6
- key_vectors: bfloat16 [12288, 4096], P('ctx', 'head'), may hold values from -11 to 11
- value_vectors: bfloat16 [12288, 4096], P('ctx', 'head'), may hold values from -6 to 6
- log_decay: float32 [12288, 4096], P('ctx', 'head'), may hold values from -0.7 to 0, as said below
- write_rate: float32 [12288, 32], P('ctx', 'head'), may hold values from 0 to 1
- out_gate: bfloat16 [12288, 4096], P('ctx', 'head'), may hold values from -6 to 6
- norm_gain: float32 [128], replicated, may hold values from 0.25 to 1.75
- out_weight: bfloat16 [4096, 2304], P('head'), may hold values from -0.09375 to 0.09375
Outputs:
- mixed: bfloat16 [12288, 2304], P(('ctx', 'head'))
Inputs may be any that keep to these rules, and one draw needn't show every extreme that they name: `log_decay`: every decay lies strictly below 1.
All inputs are finite; a program needn't handle non-finite values.
Results may differ from a plain program's by a relative error of at most 0.014.
Values may be sent and summed in bfloat16 or wider, within the bound.
A program may use at most 128 MiB of HBM per device.

v0:
```python
import jax
import jax.numpy as jnp
from jax import lax
from jax.sharding import PartitionSpec as P

HEAD_SIZE = 128
STRETCH = 64


peak_value = lax.Precision.HIGHEST


def entering(part, axis, combine, identity):
    place = lax.axis_index(axis)
    gathered = jax.tree.map(lambda a: lax.all_gather(a, axis), part)
    state = jax.tree.map(lambda a, e: jnp.zeros_like(a) + jnp.asarray(e, a.dtype), part, identity)

    def one(turn, state):
        return combine(
            state, jax.tree.map(lambda a: lax.dynamic_index_in_dim(a, turn, 0, False), gathered)
        )

    return lax.fori_loop(0, place, one, state)


def chain_mul(left_map, right_map):
    return jnp.einsum("hij,hjk->hik", left_map, right_map, precision=peak_value)


def compose_pair(earlier, later):
    return (chain_mul(later[0], earlier[0]), chain_mul(later[0], earlier[1]) + later[1])


def unit_lower_inverse(coupling):
    stretch_len = coupling.shape[-1]
    power = -coupling
    inverse = jnp.eye(stretch_len, dtype=jnp.float32) + power
    for level_index in range(1, (stretch_len - 1).bit_length()):
        power = jnp.einsum("hnts,hnsu->hntu", power, power, precision=peak_value)
        inverse = inverse + jnp.einsum("hnts,hnsu->hntu", inverse, power, precision=peak_value)
    return inverse


def on_device(
    query_vectors,
    key_vectors,
    value_vectors,
    log_decay,
    write_rate,
    out_gate,
    norm_gain,
    out_weight,
):
    row_count = query_vectors.shape[0]
    head_count = query_vectors.shape[1] // HEAD_SIZE
    block_count = row_count // STRETCH

    def arrange(source):
        return (
            source.astype(jnp.float32)
            .reshape(block_count, STRETCH, head_count, HEAD_SIZE)
            .transpose(2, 0, 1, 3)
        )

    queries = arrange(query_vectors)
    raw_keys = arrange(key_vectors)
    unit_keys = raw_keys / jnp.sqrt(jnp.sum(raw_keys * raw_keys, axis=-1, keepdims=True) + 1e-06)
    values = arrange(value_vectors)
    log_rates = arrange(log_decay)
    write_rates = write_rate.reshape(block_count, STRETCH, head_count).transpose(2, 0, 1)[..., None]
    later_pos = lax.broadcasted_iota(jnp.int32, (STRETCH, STRETCH), 0)
    earlier_pos = lax.broadcasted_iota(jnp.int32, (STRETCH, STRETCH), 1)
    lower_ones = (later_pos >= earlier_pos).astype(jnp.float32)
    strict = (later_pos > earlier_pos).astype(jnp.float32)
    cumulative = jnp.einsum("ts,hnsc->hntc", lower_ones, log_rates, precision=peak_value)
    final_log = cumulative[:, :, -1:, :]
    growth = jnp.exp(cumulative)
    key_now = unit_keys * growth
    key_back = unit_keys * jnp.exp(-cumulative)
    query_now = queries * growth
    key_end = unit_keys * jnp.exp(final_log - cumulative)
    coupling = (
        write_rates
        * jnp.einsum("hntc,hnsc->hnts", key_now, key_back, precision=peak_value)
        * strict
    )
    reading = jnp.einsum("hntc,hnsc->hnts", query_now, key_back, precision=peak_value) * lower_ones
    right_sides = jnp.concatenate([write_rates * key_now, write_rates * values], -1)
    inverse = unit_lower_inverse(coupling)
    solved = jnp.einsum("hnts,hnsd->hntd", inverse, right_sides, precision=peak_value)
    mixed_in = jnp.einsum("hnts,hnsd->hntd", reading, solved, precision=peak_value)
    query_eff = query_now - mixed_in[..., :HEAD_SIZE]
    local_part = mixed_in[..., HEAD_SIZE:]
    carried = jnp.einsum("hnsc,hnsd->hncd", key_end, solved, precision=peak_value)
    identity = jnp.eye(HEAD_SIZE, dtype=jnp.float32)
    transitions = (
        jnp.exp(final_log)[:, :, 0, :, None] * identity - carried[..., :HEAD_SIZE]
    ).transpose(1, 0, 2, 3)
    writes = carried[..., HEAD_SIZE:].transpose(1, 0, 2, 3)

    def advance(running, stretch_item):
        through, local_state = running
        step_map, step_write = stretch_item
        return (
            (chain_mul(step_map, through), chain_mul(step_map, local_state) + step_write),
            (through, local_state),
        )

    eye_heads = jnp.broadcast_to(identity, (head_count, HEAD_SIZE, HEAD_SIZE))
    zero_state = jnp.zeros((head_count, HEAD_SIZE, HEAD_SIZE), jnp.float32)
    (block_map, block_state), (start_maps, start_states) = lax.scan(
        advance, (eye_heads, zero_state), (transitions, writes)
    )
    incoming = entering((block_map, block_state), "ctx", compose_pair, (eye_heads, zero_state))[1]

    def replay(state_matrix, stretch_item):
        step_query, step_local, step_map, step_write = stretch_item
        out_rows = (
            jnp.einsum("htc,hcd->htd", step_query, state_matrix, precision=peak_value) + step_local
        )
        return (chain_mul(step_map, state_matrix) + step_write, out_rows)

    _, replayed = lax.scan(
        replay,
        incoming,
        (query_eff.transpose(1, 0, 2, 3), local_part.transpose(1, 0, 2, 3), transitions, writes),
    )
    attended = replayed.transpose(1, 0, 2, 3)
    attended = attended.transpose(1, 2, 0, 3).reshape(row_count, head_count, HEAD_SIZE)
    mean_square = jnp.mean(attended * attended, axis=-1, keepdims=True)
    gate_values = jax.nn.sigmoid(
        out_gate.astype(jnp.float32).reshape(row_count, head_count, HEAD_SIZE)
    )
    gated_out = attended / jnp.sqrt(mean_square + 1e-05) * norm_gain * gate_values
    gated_out = gated_out.astype(jnp.bfloat16).reshape(row_count, head_count * HEAD_SIZE)
    return lax.psum_scatter(
        jnp.dot(gated_out, out_weight, preferred_element_type=jnp.float32).astype(jnp.bfloat16),
        "head",
        scatter_dimension=0,
        tiled=True,
    )


def solution(mesh):
    in_specs = (
        P("ctx", "head"),
        P("ctx", "head"),
        P("ctx", "head"),
        P("ctx", "head"),
        P("ctx", "head"),
        P("ctx", "head"),
        P(),
        P("head", None),
    )
    out_specs = P(("ctx", "head"), None)
    return jax.shard_map(
        on_device, mesh=mesh, in_specs=in_specs, out_specs=out_specs, check_vma=False
    )
```

profile of v0, /device:TPU:6, one launch (start us, length us, event | category | flops | bytes accessed | tf_op | source)
XLA Modules:
  0.0 373.4 jit_solution(14264812851300034986)
XLA Ops:
  6.6 2.4 reshape.84
  9.0 1.7 fusion.29
  11.8 2.1 reshape.90
  14.0 1.6 fusion.28
  17.9 2.2 reshape.91
  20.1 2.1 reshape.92
  22.2 4.1 %broadcast_multiply_fusion = (f32[4,6,64,128]{3,0,2,1:T(4,128)S(1)}, f32[4,6,64,128]{3,0,2,1:T(4,128)S(1)}, f32[4,6,64,128]{3,0,2,1:T(4,128)S(1)}, f32[4,6,64,12...) fusion(f32[4,6,64]{0,2,1:T(8,128)} %copy.68, f32[64,4,6,128]{3,0,2,1:T(8,128)S(1)} %fusion.29, ...), kind=kLoop, calls=%fused_computation.70 | loop fusion | flops 1769472 | bytes 7888896 | tf_op jit(solution)/shard_map/mul | solution.py:88
  37.4 1.9 fusion.20
  40.5 2.8 fusion.32
  46.6 17.2 %while.39 = (s32[]{:T(128)}, f32[4,128,128]{2,1,0:T(8,128)S(1)}, f32[4,128,128]{2,1,0:T(8,128)S(1)}, f32[6,4,128,128]{3,2,1,0:T(8,128)}, f32[6,4,128,128]{3,2,1,0:T(8,128)}, /*index=5*/s32[]{:T(128)}, s32[]{:T(128)}) while((s32[]{:T(128)}, f32[4,128,128]{2,1,0:T(8,128)S(1)}, f32[4,128,128]{2,1,0:T(8,128)S(1)}, ...), condition=%wide.region_2.3_spmd.clone, body=%wide.region_1.2_spmd.clone.sunk | while | flops 201457664 | bytes 2885207 | solution.py:111
  65.3 2.8 convolution_multiply_fusion
  68.2 1.5 fusion.55
  70.9 1.5 fusion.27
  72.3 91.6 %all-gather.5.cloned.1.call-done = f32[128,128,128]{2,1,0:T(8,128)} async-done(((f32[4,128,128]{2,1,0:T(8,128)}), f32[128,128,128]{2,1,0:T(8,128)}) %all-gather.5.cloned.1.call-update) | async-done | bytes 8388624 | tf_op jit(solution)/shard_map/all_gather | solution.py:15
  164.0 98.0 %all-gather.7.cloned.1.call-done = f32[128,128,128]{2,1,0:T(8,128)} async-done(((f32[4,128,128]{2,1,0:T(8,128)}), f32[128,128,128]{2,1,0:T(8,128)}) %all-gather.7.cloned.1.call-update) | async-done | bytes 8388624 | tf_op jit(solution)/shard_map/all_gather | solution.py:15
  262.0 35.7 %while.37 = (s32[]{:T(128)}, f32[4,128,128]{2,1,0:T(8,128)S(1)}, s32[]{:T(128)}, f32[32,4,128,128]{3,2,1,0:T(8,128)}, f32[32,4,128,128]{3,2,1,0:T(8,128)}, /*index=5*/s32[]{:T(128)}, s32[]{:T(128)}, s32[]{:T(128)}) while((s32[]{:T(128)}, f32[4,128,128]{2,1,0:T(8,128)S(1)}, s32[]{:T(128)}, f32[32,4,128,128]{3,2,1,0:T(8,128)}, ...), condition=%wide.region_4.5_spmd, body=%wide.region_3.4_spmd.sunk | while | flops 100728832 | bytes 1574007 | solution.py:23
  262.0 1.4 convolution_add_fusion.12
  265.0 1.4 convolution_add_fusion.12
  269.5 1.4 convolution_add_fusion.12
  293.3 1.4 convolution_add_fusion.12
  297.7 22.3 %while.38 = (s32[]{:T(128)}, f32[4,128,128]{2,1,0:T(8,128)S(1)}, f32[6,4,64,128]{3,2,1,0:T(8,128)S(1)}, f32[6,4,128,128]{3,2,1,0:T(8,128)}, f32[6,4,128,128]{3,2...) while((s32[]{:T(128)}, f32[4,128,128]{2,1,0:T(8,128)S(1)}, ...), condition=%wide.region_6.7_spmd, body=%wide.region_5.6_spmd.sunk | while | flops 151093248 | bytes 2491485 | solution.py:123
  300.2 1.4 convolution_add_fusion.13
  321.5 2.5 convolution_convert_fusion
  324.1 42.8 %reduce-scatter.2.cloned.1.call-done = bf16[48,2304]{1,0:T(8,128)(2,1)} async-done(((bf16[384,2304]{1,0:T(8,128)(2,1)}), bf16[48,2304]{1,0:T(8,128)(2,1)}) %reduce-scatter.2.cloned.1.call-update) | async-done | bytes 221200 | tf_op jit(solution)/shard_map/reduce_scatter | solution.py:136
  (153 shorter events, 89.3 us)
Async XLA Ops:
  6.5 315.0 %copy-start = (bf16[512,2304]{1,0:T(8,128)(2,1)S(1)}, bf16[512,2304]{1,0:T(8,128)(2,1)}, u32[]{:S(2)}) copy-start(bf16[512,2304]{1,0:T(8,128)(2,1)} %param.21) | copy-start | bytes 7077892
  6.5 157.4 %all-gather.5.cloned.1.call-start = ((), (), s32[]{:S(2)}) async-start(), calls=%async_computation.2 | async-start | bytes 8650752 | tf_op jit(solution)/shard_map/all_gather | solution.py:15
  26.3 2.3 copy-start.6
  35.1 1.0 copy-start.7
  39.3 1.2 copy-start.1
  46.6 18.8 %copy-start.8 = (f32[128]{0:T(128)S(1)}, f32[128]{0:T(128)}, u32[]{:S(2)}) copy-start(f32[128]{0:T(128)} %param.20) | copy-start | bytes 1540
  63.7 0.7 copy-start.3
  63.7 0.8 copy-start.4
  64.5 197.5 %all-gather.7.cloned.1.call-start = ((), (), s32[]{:S(2)}) async-start(), calls=%async_computation.3 | async-start | bytes 8650752 | tf_op jit(solution)/shard_map/all_gather | solution.py:15
  65.2 301.6 %reduce-scatter.2.cloned.1.call-start = ((), (), s32[]{:S(2)}) async-start(), calls=%async_computation.1 | async-start | bytes 1990656 | tf_op jit(solution)/shard_map/reduce_scatter | solution.py:136
  65.3 2.9 copy-start.2
  69.7 1.2 copy-start.5
  320.5 1.0 copy-start.9
Sparse Core Ops, SparseCore 0:
  64.6 99.3 all-gather.4
  166.5 95.3 all-gather.6
  324.2 42.6 reduce-scatter.1
where the time goes:
time: 375 us; the launch traced here: 373 us
  waiting for transfers between devices  233 us (62%)
  matrix products  91 us (24%)
  local copies, waits for them, and re-layouts  24.7 us (7%)
  between operations  13.5 us (4%)
  other arithmetic  9.24 us (2%)
    all_gather x2, waiting for transfers between devices, entering(): gathered = jax.tree.map(lambda a: lax.all_gather(a, axis), part)  190 us
    dot_general x42, matrix products, chain_mul(): return jnp.einsum('hij,hjk->hik', left_map, right_map, precision=peak_value)  59.5 us
    reduce_scatter x1, waiting for transfers between devices, on_device(): lax.psum_scatter(jnp.dot(gated_out, out_weight, preferred_element_type=jn...  42.8 us
    dot_general x6, matrix products, replay(): jnp.einsum('htc,hcd->htd', step_query, state_matrix, precision=peak_value)  7.64 us
  transfers between devices with their start and end apart: 3, of which 3 were waited for; matrix products, arithmetic and copies ran while one was open for 2% of the time, Pallas kernels for 0%

commit v1 on v0

v1 whole, which is shorter than its diff:
```python
import jax
import jax.numpy as jnp
from jax import lax
from jax.experimental import pallas as pl
from jax.experimental.pallas import tpu as pltpu
from jax.sharding import PartitionSpec as P

HS = 128
C = 64
NX, NZ = 4, 8
NY, NC = 4, 2
MSG = 208
HALF = HS // 2
MESH = pl.DeviceIdType.MESH
bf16, f32 = jnp.bfloat16, jnp.float32
NN, NT, TN = ((1,), (0,)), ((1,), (1,)), ((0,), (0,))


def mm(a, b, dims=NN):
    return lax.dot_general(
        a.astype(bf16), b.astype(bf16), (dims, ((), ())), preferred_element_type=f32
    )


def prep_kernel(q_ref, k_ref, v_ref, ld_ref, wr_ref, qd_ref, loc_ref, msg_ref):
    h = pl.program_id(0)
    rows = q_ref.shape[0]
    n = rows // C
    kf = k_ref[...].astype(f32)
    unit = kf * lax.rsqrt(jnp.sum(kf * kf, axis=-1, keepdims=True) + 1e-6)
    wr = wr_ref[...]
    lane = lax.broadcasted_iota(jnp.int32, wr.shape, 1)
    beta = jnp.sum(jnp.where(lane == h, wr, 0.0), axis=1, keepdims=True)
    i = lax.broadcasted_iota(jnp.int32, (C, C), 0)
    j = lax.broadcasted_iota(jnp.int32, (C, C), 1)
    lower = (i >= j).astype(bf16)
    eye = (i == j).astype(f32)
    ei = lax.broadcasted_iota(jnp.int32, (HS, HS), 0)
    ej = lax.broadcasted_iota(jnp.int32, (HS, HS), 1)
    ld = ld_ref[...]
    hi = ld.astype(bf16)
    lo = (ld - hi.astype(f32)).astype(bf16)
    parts = []
    for c in range(n):
        s = slice(c * C, (c + 1) * C)
        cum = mm(lower, hi[s]) + mm(lower, lo[s])
        end = cum[C - 1 : C]
        grow = jnp.exp(cum)
        kn = beta[s] * (unit[s] * grow)
        qn = q_ref[s].astype(f32) * grow
        kb = unit[s] * jnp.exp(-cum)
        ke = unit[s] * jnp.exp(end - cum)
        ar = mm(jnp.concatenate([kn, qn], 0), kb, NT)
        coupling = jnp.where(i > j, ar[:C], 0.0)
        reading = jnp.where(i >= j, ar[C:], 0.0)
        inv = eye
        b = 1
        while b < C:
            mask = ((i // b) % 2 == 1) & ((j // b) == (i // b) - 1)
            step = jnp.where(mask, coupling, 0.0)
            inv = inv - (step if b == 1 else mm(inv, mm(step, inv)))
            b *= 2
        y = mm(inv, jnp.concatenate([kn, beta[s] * v_ref[s].astype(f32)], 1))
        ry = mm(reading, y)
        parts.append((qn - ry[:, :HS], ry[:, HS:], mm(y, ke, TN), jnp.exp(end)))
    x = jnp.concatenate([(ei == ej).astype(f32), jnp.zeros((HS, HS), f32)], 0)
    total = jnp.ones((1, HS), f32)
    for c in range(n):
        s = slice(c * C, (c + 1) * C)
        qe, rl, yk, d = parts[c]
        o = mm(qe, x, NT)
        qd_ref[s] = o[:, :HS].astype(bf16)
        loc_ref[s] = o[:, HS:] + rl
        nx = x * d - mm(x, yk[:HS])
        x = jnp.concatenate([nx[:HS], nx[HS:] + yk[HS:]], 0)
        total = total * d
    take = jnp.where(ei == ej, total, 0.0) - x[:HS]
    d1 = total.astype(bf16).astype(f32)
    d2 = (total - d1).astype(bf16).astype(f32)
    d3 = total - d1 - d2
    ti = lax.broadcasted_iota(jnp.int32, (MSG - HS - HALF, HS), 0)
    tail = jnp.where(ti == 0, d1, jnp.where(ti == 1, d2, jnp.where(ti == 2, d3, 0.0)))
    for c in range(2):
        msg_ref[c, :HS] = take.astype(bf16)
        msg_ref[c, HS : HS + HALF] = x[HS + c * HALF : HS + (c + 1) * HALF].astype(bf16)
        msg_ref[c, HS + HALF :] = tail.astype(bf16)


def mix_kernel(
    msg_ref,
    qd_ref,
    loc_ref,
    gate_ref,
    gain_ref,
    w_ref,
    out_ref,
    rmsg,
    pre,
    s0_out,
    s0_in,
    sin_out,
    sin,
    gated,
    gsib,
    weights,
    psend,
    precv,
    own,
    m_send,
    m_recv,
    x_send,
    x_recv,
    s_send,
    s_recv,
    g_send,
    g_recv,
    w_sem,
    w_send,
    w_recv,
    p_send,
    p_recv,
):
    ctx = lax.axis_index("ctx")
    head = lax.axis_index("head")
    x, z = ctx // NZ, ctx % NZ
    y, core = head // NC, head % NC
    kd = w_ref.shape[0]
    rows = qd_ref.shape[0] // (NY * NC)
    width = w_ref.shape[1]
    sib = (ctx, y * NC + (1 - core))

    def zdev(zz):
        return (x * NZ + zz, head)

    def ydev(yy):
        return (ctx, yy * NC + core)

    xnext = (lax.rem(x + 1, NX) * NZ + z, head)
    xprev = (lax.rem(x + NX - 1, NX) * NZ + z, head)
    barrier = pltpu.get_barrier_semaphore()
    peers = [zdev(lax.rem(z + s, NZ)) for s in range(1, NZ)]
    peers += [ydev(lax.rem(y + s, NY)) for s in range(1, NY)]
    peers += [sib, xnext, xprev]
    for peer in peers:
        pl.semaphore_signal(barrier, inc=1, device_id=peer, device_id_type=MESH)
    pl.semaphore_wait(barrier, len(peers))

    def remote(src, dst, send, recv, dev):
        return pltpu.make_async_remote_copy(
            src_ref=src, dst_ref=dst, send_sem=send, recv_sem=recv, device_id=dev, device_id_type=MESH
        )

    started = []
    for s in range(1, NZ):
        zz = lax.rem(z + s, NZ)
        cp = remote(msg_ref.at[zz], rmsg.at[z], m_send.at[s], m_recv.at[z], zdev(zz))
        cp.start()
        started.append(cp)
    rmsg[z] = msg_ref[z]
    wown = pltpu.make_async_copy(w_ref, weights.at[core], w_sem)
    wown.start()
    wsib = remote(w_ref, weights.at[core], w_send, w_recv, sib)
    wsib.start()

    ei = lax.broadcasted_iota(jnp.int32, (HS + HALF, HS), 0)
    ej = lax.broadcasted_iota(jnp.int32, (HS + HALF, HS), 1)
    run = (ei == ej).astype(f32)
    for zz in range(NZ):

        @pl.when(z != zz)
        def _(zz=zz):
            remote(msg_ref.at[0], rmsg.at[zz], m_send.at[0], m_recv.at[zz], zdev(zz)).wait_recv()

        pre[zz] = run
        d = jnp.sum(rmsg[zz, HS + HALF :, :].astype(f32), axis=0, keepdims=True)
        new = run * d - mm(run, rmsg[zz, :HS, :])
        run = jnp.concatenate([new[:HS], new[HS:] + rmsg[zz, HS : HS + HALF, :].astype(f32)], 0)

    chain = remote(s0_out, s0_in, x_send, x_recv, xnext)

    @pl.when(x == 0)
    def _():
        s0_in[...] = jnp.zeros_like(s0_in)

    @pl.when(x > 0)
    def _():
        remote(s0_out, s0_in, x_send, x_recv, xprev).wait_recv()

    s0 = s0_in[...]

    @pl.when(x < NX - 1)
    def _():
        s0_out[...] = mm(s0, run[:HS]) + run[HS:]
        chain.start()

    for s in range(1, NZ):
        zz = lax.rem(z + s, NZ)
        sin_out[zz] = (mm(s0, pre[zz, :HS, :]) + pre[zz, HS:, :]).astype(bf16)
        cp = remote(sin_out.at[zz], sin.at[z], s_send.at[s], s_recv.at[z], zdev(zz))
        cp.start()
        started.append(cp)
    sin[z] = (mm(s0, pre[z, :HS, :]) + pre[z, HS:, :]).astype(bf16)

    gcopies = []
    for hh in range(qd_ref.shape[1] // HS):
        for half in range(2):
            slot = 2 * hh + half

            @pl.when(z != slot)
            def _(slot=slot):
                remote(sin_out.at[0], sin.at[slot], s_send.at[0], s_recv.at[slot], zdev(slot)).wait_recv()

        state = jnp.concatenate([sin[2 * hh], sin[2 * hh + 1]], 0)
        cols = slice(hh * HS, (hh + 1) * HS)
        att = mm(qd_ref[:, cols], state, NT) + loc_ref[:, cols]
        ms = jnp.mean(att * att, axis=-1, keepdims=True)
        gate = jax.nn.sigmoid(gate_ref[:, cols].astype(f32))
        g = (att * lax.rsqrt(ms + 1e-5) * gain_ref[...] * gate).astype(bf16)
        for jj in range(NY * NC):
            gated[jj % NC, jj // NC, :, cols] = g[jj * rows : (jj + 1) * rows]
        cp = remote(
            gated.at[1 - core, :, :, cols], gsib.at[:, :, cols], g_send.at[hh], g_recv.at[hh], sib
        )
        cp.start()
        gcopies.append(cp)

    wown.wait()
    wsib.wait()
    for cp in gcopies:
        cp.wait()
    mine = gated[core].reshape(NY * rows, kd)
    other = gsib[...].reshape(NY * rows, kd)
    tile = 768
    for nt in range(width // tile):
        cols = slice(nt * tile, (nt + 1) * tile)
        acc = mm(mine, weights[core, :, cols]) + mm(other, weights[1 - core, :, cols])
        psend[:, :, cols] = acc.reshape(NY, rows, tile).astype(bf16)
        for s in (2, 1, 3):
            yy = lax.rem(y + s, NY)
            cp = remote(
                psend.at[yy, :, cols],
                precv.at[y, :, cols],
                p_send.at[s, nt],
                p_recv.at[y, nt],
                ydev(yy),
            )
            cp.start()
            started.append(cp)
    for nt in range(width // tile):
        cols = slice(nt * tile, (nt + 1) * tile)
        total = psend[y, :, cols].astype(f32)
        for s in range(1, NY):
            yy = lax.rem(y + s, NY)
            remote(
                psend.at[0, :, cols],
                precv.at[yy, :, cols],
                p_send.at[0, nt],
                p_recv.at[yy, nt],
                ydev(yy),
            ).wait_recv()
            total = total + precv[yy, :, cols].astype(f32)
        out_ref[:, cols] = total.astype(bf16)

    @pl.when(x < NX - 1)
    def _():
        chain.wait_send()

    for cp in started:
        cp.wait_send()


def on_device(q, k, v, ld, wr, gate, gain, w):
    rows, feats = q.shape
    heads = feats // HS
    blk = pl.BlockSpec((rows, HS), lambda h: (0, h))
    qd, loc, msg = pl.pallas_call(
        prep_kernel,
        grid=(heads,),
        in_specs=[blk, blk, blk, blk, pl.BlockSpec(wr.shape, lambda h: (0, 0))],
        out_specs=[blk, blk, pl.BlockSpec((2, MSG, HS), lambda h: (h, 0, 0))],
        out_shape=[
            jax.ShapeDtypeStruct((rows, feats), bf16),
            jax.ShapeDtypeStruct((rows, feats), f32),
            jax.ShapeDtypeStruct((2 * heads, MSG, HS), bf16),
        ],
        compiler_params=pltpu.CompilerParams(vmem_limit_bytes=32 << 20),
        name="prep",
    )(q, k, v, ld, wr)
    kd, width = w.shape
    rb = rows // (NY * NC)
    vm = pl.BlockSpec(memory_space=pltpu.VMEM)
    dma = pltpu.SemaphoreType.DMA
    nt = width // 768
    return pl.pallas_call(
        mix_kernel,
        in_specs=[vm, vm, vm, vm, vm, pl.BlockSpec(memory_space=pl.ANY)],
        out_specs=vm,
        out_shape=jax.ShapeDtypeStruct((rb, width), bf16),
        scratch_shapes=[
            pltpu.VMEM((NZ, MSG, HS), bf16),
            pltpu.VMEM((NZ, HS + HALF, HS), f32),
            pltpu.VMEM((HALF, HS), f32),
            pltpu.VMEM((HALF, HS), f32),
            pltpu.VMEM((NZ, HALF, HS), bf16),
            pltpu.VMEM((NZ, HALF, HS), bf16),
            pltpu.VMEM((NC, NY, rb, kd), bf16),
            pltpu.VMEM((NY, rb, kd), bf16),
            pltpu.VMEM((NC, kd, width), bf16),
            pltpu.VMEM((NY, rb, width), bf16),
            pltpu.VMEM((NY, rb, width), bf16),
            pltpu.VMEM((8, HS), f32),
            dma((NZ,)),
            dma((NZ,)),
            dma,
            dma,
            dma((NZ,)),
            dma((NZ,)),
            dma((heads,)),
            dma((heads,)),
            dma,
            dma,
            dma,
            dma((NY, nt)),
            dma((NY, nt)),
        ],
        compiler_params=pltpu.CompilerParams(
            collective_id=0, has_side_effects=True, vmem_limit_bytes=48 << 20
        ),
        name="mix",
    )(msg, qd, loc, gate, gain.reshape(1, HS), w)


def solution(mesh):
    in_specs = (
        P("ctx", "head"),
        P("ctx", "head"),
        P("ctx", "head"),
        P("ctx", "head"),
        P("ctx", "head"),
        P("ctx", "head"),
        P(),
        P("head", None),
    )
    out_specs = P(("ctx", "head"), None)
    return jax.shard_map(
        on_device, mesh=mesh, in_specs=in_specs, out_specs=out_specs, check_vma=False
    )
```

time: 375 us -> 101 us (0.27)
  waiting for transfers between devices: 233 us -> 0 us
  Pallas kernels: 0 us -> 93.1 us
  matrix products: 91 us -> 0 us
  local copies, waits for them, and re-layouts: 24.7 us -> 7.42 us
  between operations: 13.5 us -> 0.05 us
  other arithmetic: 9.24 us -> 0 us
    all_gather x2 -> x0, waiting for transfers between devices: 190 us -> none  [entering(): gathered = jax.tree.map(lambda a: lax.all_gather(a, axis), part)]
    pallas_call x0 -> x2, Pallas kernels: none -> 93.1 us  [the longest x1 49.8 us: on_device(): pl.pallas_call(mix_kernel, in_specs=[vm, vm, vm, vm, vm, pl.BlockSpec(mem...]
    dot_general x65 -> x0, matrix products: 91 us -> none  [the longest x42 59.5 us: chain_mul(): return jnp.einsum('hij,hjk->hik', left_map, right_map, precision=peak_value)]
    reduce_scatter x1 -> x0, waiting for transfers between devices: 42.8 us -> none  [on_device(): lax.psum_scatter(jnp.dot(gated_out, out_weight, preferred_element_type=jn...]
    transpose x5 -> x0, local copies, waits for them, and re-layouts: 8.34 us -> none  [the longest x3 6.42 us: arrange(): return source.astype(jnp.float32).reshape(block_count, STRETCH, head_coun...]
    dynamic_slice x6 -> x0, local copies, waits for them, and re-layouts: 5.5 us -> none  [on_device(): lax.scan(replay, incoming, (query_eff.transpose(1, 0, 2, 3), local_part.t...]
    mul x1 -> x0, other arithmetic: 4.1 us -> none  [on_device(): write_rates * key_now]
  transfers between devices with their start and end apart: 3 -> 0, of which waited for: 3 -> 0; matrix products, arithmetic and copies ran while one was open for 2% -> 0% of each run, Pallas kernels for 0% -> 0%
where the time goes in v1:
time: 101 us
  Pallas kernels  93.1 us (92%)
  local copies, waits for them, and re-layouts  7.42 us (7%)
    pallas_call x1, Pallas kernels, on_device(): pl.pallas_call(mix_kernel, in_specs=[vm, vm, vm, vm, vm, pl.BlockSpec(mem...  49.8 us
    pallas_call x1, Pallas kernels, on_device(): pl.pallas_call(prep_kernel, grid=(heads,), in_specs=[blk, blk, blk, blk,...  43.2 us
    unnamed x16, local copies, waits for them, and re-layouts  7.42 us

profile of v1, /device:TPU:6, one launch (start us, length us, event | category | flops | bytes accessed | tf_op | source)
XLA Modules:
  0.0 100.5 jit_solution(12715860241556062816)
XLA Ops:
  0.0 0.0 copy-start
  0.0 1.0 copy.9.wr_ref
  1.0 0.0 copy-start.1
  1.0 1.1 %copy-done.1 = f32[384,512]{1,0:T(8,128)S(1)} copy-done((f32[384,512]{1,0:T(8,128)S(1)}, f32[384,512]{1,0:T(8,128)}, u32[]{:S(2)}) %copy-start.1) | copy-done | bytes 786456
  2.1 0.0 copy-start.3
  2.1 1.0 copy-done.3
  3.1 0.0 copy-start.4
  3.1 1.0 copy-done.4
  4.1 0.0 copy-start.5
  4.1 1.0 copy-done.5
  5.1 43.2 %prep.1 = (bf16[384,512]{1,0:T(8,128)(2,1)S(1)}, f32[384,512]{1,0:T(8,128)S(1)}, bf16[8,208,128]{2,1,0:T(8,128)(2,1)S(1)}) custom-call(bf16[384,512]{1,0:T(8,128)(2,1)S(1)} %copy-done.3, bf16[384,512]{1,0:T(8,128)(2,1)S(1)} %copy-done.4, bf16[384,512]{1,0:T(8,128)(2,1)S(1)} %copy-done.5, f32[384,512]{1,0:T(8,128)S(1)} %copy-done.1, f32[384,4]{1,0:T(8,128)S(1)} %copy.9.wr_ref), custom_call_target="tpu_custom_call" | custom-call | tf_op jit(solution)/shard_map/prep/pallas_call | solution.py:276
  48.3 0.0 copy-done
  48.4 0.0 copy-start.2
  48.4 1.0 copy-done.2
  49.4 0.0 copy-start.6
  49.4 0.7 copy-done.6
  50.0 49.8 %mix.1 = bf16[48,2304]{1,0:T(8,128)(2,1)S(1)} custom-call(bf16[8,208,128]{2,1,0:T(8,128)(2,1)S(1)} %get-tuple-element.8.msg_ref, bf16[384,512]{1,0:T(8,128)(2,1)S(1)} %get-tuple-element.9.qd_ref, f32[384,512]{1,0:T(8,128)S(1)} %get-tuple-element.10.loc_ref, bf16[384,512]{1,0:T(8,128)(2,1)S(1)} %copy-done.2, f32[1,128]{1,0:T(1,128)S(1)} %bitcast.1, ...), custom_call_target="tpu_custom_call" | custom-call | tf_op jit(solution)/shard_map/mix/pallas_call | solution.py:294
  99.8 0.7 copy.11
Async XLA Ops:
  0.0 48.3 %copy-start = (bf16[512,2304]{1,0:T(8,128)(2,1)S(1)}, bf16[512,2304]{1,0:T(8,128)(2,1)}, u32[]{:S(2)}) copy-start(bf16[512,2304]{1,0:T(8,128)(2,1)} %w_ref.1) | copy-start | bytes 7077892
  1.0 1.1 %copy-start.1 = (f32[384,512]{1,0:T(8,128)S(1)}, f32[384,512]{1,0:T(8,128)}, u32[]{:S(2)}) copy-start(f32[384,512]{1,0:T(8,128)} %ld_ref.1) | copy-start | bytes 2359300
  2.1 1.0 copy-start.3
  3.1 1.0 copy-start.4
  4.1 1.0 copy-start.5
  48.4 1.0 copy-start.2
  49.4 0.7 copy-start.6

commit v2 on v1

v2 whole, which is shorter than its diff:
```python
import jax
import jax.numpy as jnp
from jax import lax
from jax.experimental import pallas as pl
from jax.experimental.pallas import tpu as pltpu
from jax.sharding import PartitionSpec as P

HS = 128
C = 64
W = 2 * C
NX, NZ = 4, 8
NY, NC = 4, 2
MSG = 208
HALF = HS // 2
NT_OUT = 6
MESH = pl.DeviceIdType.MESH
bf16, f32 = jnp.bfloat16, jnp.float32
NN, NT, TN = ((1,), (0,)), ((1,), (1,)), ((0,), (0,))


def mm(a, b, dims=NN):
    return lax.dot_general(
        a.astype(bf16), b.astype(bf16), (dims, ((), ())), preferred_element_type=f32
    )


def prep(heads):
    i = lax.broadcasted_iota(jnp.int32, (W, W), 0)
    j = lax.broadcasted_iota(jnp.int32, (W, W), 1)
    lower = ((i >= j) & ((i // C) == (j // C))).astype(bf16)
    eye = (i == j).astype(f32)
    zero = jnp.zeros((W, W), bf16)
    blocks = []
    for q, k, v, ld, beta in heads:
        n = q.shape[0] // W
        for p in range(n):
            s = slice(p * W, (p + 1) * W)
            blocks.append(dict(q=q[s], k=k[s], v=v[s], ld=ld[s], beta=beta[s]))
    for b in blocks:
        hi = b["ld"].astype(bf16)
        lo = (b["ld"] - hi.astype(f32)).astype(bf16)
        b["cum"] = mm(lower, hi) + mm(lower, lo)
    for b in blocks:
        kf = b["k"].astype(f32)
        unit = kf * lax.rsqrt(jnp.sum(kf * kf, axis=-1, keepdims=True) + 1e-6)
        cum = b.pop("cum")
        e1, e2 = cum[C - 1 : C], cum[W - 1 : W]
        d1, d2 = jnp.exp(e1), jnp.exp(e2)
        grow = jnp.exp(cum)
        back = (unit * jnp.exp(-cum)).astype(bf16)
        kn = b["beta"] * (unit * grow)
        qn = b["q"].astype(f32) * grow
        ke1 = unit[:C] * jnp.exp(e1 - cum[:C])
        ke2 = unit[C:] * jnp.exp(e2 - cum[C:])
        knb, qnb = kn.astype(bf16), qn.astype(bf16)
        top = mm(jnp.concatenate([knb[:C], qnb[:C]], 0), back, NT)
        earlier = jnp.concatenate([ke1.astype(bf16), back[C:]], 0)
        bot = mm(jnp.concatenate([knb[C:], qnb[C:]], 0), earlier, NT)
        b["a"] = jnp.where(i > j, jnp.concatenate([top[:C], bot[:C]], 0), 0.0).astype(bf16)
        b["r"] = jnp.where(i >= j, jnp.concatenate([top[C:], bot[C:]], 0), 0.0).astype(bf16)
        b["qn"] = jnp.concatenate([qn[:C], qn[C:] * d1], 0)
        left = jnp.concatenate([knb[:C], (kn[C:] * d1).astype(bf16)], 0)
        right = (b["beta"] * b["v"].astype(f32)).astype(bf16)
        b["rhs"] = jnp.concatenate([left, right], 1)
        b["ke"] = jnp.concatenate([(ke1 * d2).astype(bf16), ke2.astype(bf16)], 0)
        b["d"] = d1 * d2
    size = 1
    while size < W:
        mask = ((i // size) % 2 == 1) & ((j // size) == (i // size) - 1)
        for b in blocks:
            step = jnp.where(mask, b["a"], zero)
            b["st"] = step if size == 1 else mm(step, b["t"]).astype(bf16)
        for b in blocks:
            b["t"] = eye - b["st"].astype(f32) if size == 1 else b["t"] - mm(b["t"], b["st"])
        size *= 2
    for b in blocks:
        b["y"] = mm(b["t"], b["rhs"]).astype(bf16)
    for b in blocks:
        b["ry"] = mm(b["r"], b["y"])
    for b in blocks:
        b["yk"] = mm(b["y"], b["ke"], TN)
    n = len(blocks) // len(heads)
    x = [None for _ in heads]
    total = [None for _ in heads]
    qd = [[] for _ in heads]
    loc = [[] for _ in heads]
    for p in range(n):
        for h in range(len(heads)):
            b = blocks[h * n + p]
            qe = b["qn"] - b["ry"][:, :HS]
            if p == 0:
                qd[h].append(qe.astype(bf16))
                loc[h].append(b["ry"][:, HS:])
                x[h] = jnp.concatenate([eye * b["d"] - b["yk"][:HS], b["yk"][HS:]], 0)
                total[h] = b["d"]
            else:
                xb = x[h].astype(bf16)
                o = mm(qe, xb, NT)
                qd[h].append(o[:, :HS].astype(bf16))
                loc[h].append(o[:, HS:] + b["ry"][:, HS:])
                nx = x[h] * b["d"] - mm(xb, b["yk"][:HS])
                x[h] = jnp.concatenate([nx[:HS], nx[HS:] + b["yk"][HS:]], 0)
                total[h] = total[h] * b["d"]
    return [
        (qd[h], loc[h], eye * total[h] - x[h][:HS], x[h][HS:], total[h]) for h in range(len(heads))
    ]


def kernel(
    q_hbm,
    k_hbm,
    v_hbm,
    ld_hbm,
    wr_hbm,
    gate_hbm,
    gain_hbm,
    w_hbm,
    out_ref,
    q_ref,
    k_ref,
    v_ref,
    ld_ref,
    wr_ref,
    gate_ref,
    gain_ref,
    qd_ref,
    loc_ref,
    msg_ref,
    rmsg,
    pre,
    s0_out,
    s0_in,
    sin_out,
    sin,
    gated,
    gsib,
    weights,
    acc,
    psend,
    pvia,
    precv,
    in_sem,
    m_send,
    m_recv,
    x_send,
    x_recv,
    s_send,
    s_recv,
    g_send,
    g_recv,
    w_sem,
    w_send,
    w_recv,
    p_send,
    v_recv,
    p_recv,
):
    ctx = lax.axis_index("ctx")
    head = lax.axis_index("head")
    x, z = ctx // NZ, ctx % NZ
    y, core = head // NC, head % NC
    feats = qd_ref.shape[1]
    heads = feats // HS
    rows = qd_ref.shape[0] // (NY * NC)
    sib = (ctx, y * NC + (1 - core))

    def zdev(zz):
        return (x * NZ + zz, head)

    ynext = (ctx, lax.rem(y + 1, NY) * NC + core)
    yprev = (ctx, lax.rem(y + NY - 1, NY) * NC + core)
    xnext = (lax.rem(x + 1, NX) * NZ + z, head)
    xprev = (lax.rem(x + NX - 1, NX) * NZ + z, head)
    barrier = pltpu.get_barrier_semaphore()
    peers = [zdev(lax.rem(z + s, NZ)) for s in range(1, NZ)] + [ynext, yprev, sib, xnext, xprev]
    for peer in peers:
        pl.semaphore_signal(barrier, inc=1, device_id=peer, device_id_type=MESH)

    loads = []
    for n, (src, dst) in enumerate(
        (
            (ld_hbm, ld_ref),
            (k_hbm, k_ref),
            (wr_hbm, wr_ref),
            (q_hbm, q_ref),
            (v_hbm, v_ref),
            (gate_hbm, gate_ref),
            (gain_hbm, gain_ref),
        )
    ):
        cp = pltpu.make_async_copy(src, dst, in_sem.at[n])
        cp.start()
        loads.append(cp)
    wown = pltpu.make_async_copy(w_hbm, weights.at[core], w_sem)
    wown.start()
    for cp in loads:
        cp.wait()

    def remote(src, dst, send, recv, dev):
        return pltpu.make_async_remote_copy(
            src_ref=src, dst_ref=dst, send_sem=send, recv_sem=recv, device_id=dev, device_id_type=MESH
        )

    beta = wr_ref[...].T
    args = []
    for h in range(heads):
        cols = slice(h * HS, (h + 1) * HS)
        args.append((q_ref[:, cols], k_ref[:, cols], v_ref[:, cols], ld_ref[:, cols], beta[:, h : h + 1]))
    ti = lax.broadcasted_iota(jnp.int32, (MSG - HS - HALF, HS), 0)
    for h, (qd, loc, take, state, total) in enumerate(prep(args)):
        cols = slice(h * HS, (h + 1) * HS)
        for p in range(len(qd)):
            qd_ref[p * W : (p + 1) * W, cols] = qd[p]
            loc_ref[p * W : (p + 1) * W, cols] = loc[p]
        t1 = total.astype(bf16).astype(f32)
        t2 = (total - t1).astype(bf16).astype(f32)
        t3 = total - t1 - t2
        tail = jnp.where(ti == 0, t1, jnp.where(ti == 1, t2, jnp.where(ti == 2, t3, 0.0)))
        for c in range(2):
            msg_ref[2 * h + c, :HS] = take.astype(bf16)
            msg_ref[2 * h + c, HS : HS + HALF] = state[c * HALF : (c + 1) * HALF].astype(bf16)
            msg_ref[2 * h + c, HS + HALF :] = tail.astype(bf16)

    pl.semaphore_wait(barrier, len(peers))

    started = []
    for s in (4, 3, 5, 2, 6, 1, 7):
        zz = lax.rem(z + s, NZ)
        cp = remote(msg_ref.at[zz], rmsg.at[z], m_send.at[s], m_recv.at[z], zdev(zz))
        cp.start()
        started.append(cp)
    wsib = remote(w_hbm, weights.at[core], w_send, w_recv, sib)
    wsib.start()
    rmsg[z] = msg_ref[z]

    ei = lax.broadcasted_iota(jnp.int32, (HS + HALF, HS), 0)
    ej = lax.broadcasted_iota(jnp.int32, (HS + HALF, HS), 1)
    run = (ei == ej).astype(f32)
    for zz in range(NZ):

        @pl.when(z != zz)
        def _(zz=zz):
            remote(msg_ref.at[0], rmsg.at[zz], m_send.at[0], m_recv.at[zz], zdev(zz)).wait_recv()

        pre[zz] = run
        d = jnp.sum(rmsg[zz, HS + HALF :, :].astype(f32), axis=0, keepdims=True)
        new = run * d - mm(run, rmsg[zz, :HS, :])
        run = jnp.concatenate([new[:HS], new[HS:] + rmsg[zz, HS : HS + HALF, :].astype(f32)], 0)

    chain = remote(s0_out, s0_in, x_send, x_recv, xnext)

    @pl.when(x == 0)
    def _():
        s0_in[...] = jnp.zeros_like(s0_in)

    @pl.when(x > 0)
    def _():
        remote(s0_out, s0_in, x_send, x_recv, xprev).wait_recv()

    s0 = s0_in[...]

    @pl.when(x < NX - 1)
    def _():
        s0_out[...] = (mm(s0, run[:HS]) + run[HS:]).astype(bf16)
        chain.start()

    for s in (4, 3, 5, 2, 6, 1, 7):
        zz = lax.rem(z + s, NZ)
        sin_out[zz] = (mm(s0, pre[zz, :HS, :]) + pre[zz, HS:, :]).astype(bf16)
        cp = remote(sin_out.at[zz], sin.at[z], s_send.at[s], s_recv.at[z], zdev(zz))
        cp.start()
        started.append(cp)
    sin[z] = (mm(s0, pre[z, :HS, :]) + pre[z, HS:, :]).astype(bf16)

    gcopies = []
    for hh in range(heads):
        for slot in (2 * hh, 2 * hh + 1):

            @pl.when(z != slot)
            def _(slot=slot):
                remote(sin_out.at[0], sin.at[slot], s_send.at[0], s_recv.at[slot], zdev(slot)).wait_recv()

        state = jnp.concatenate([sin[2 * hh], sin[2 * hh + 1]], 0)
        cols = slice(hh * HS, (hh + 1) * HS)
        att = mm(qd_ref[:, cols], state, NT) + loc_ref[:, cols]
        ms = jnp.mean(att * att, axis=-1, keepdims=True)
        gate = jax.nn.sigmoid(gate_ref[:, cols].astype(f32))
        g = (att * lax.rsqrt(ms + 1e-5) * gain_ref[...] * gate).astype(bf16)
        for jj in range(NY * NC):
            gated[jj % NC, jj // NC, :, cols] = g[jj * rows : (jj + 1) * rows]
        cp = remote(
            gated.at[1 - core, :, :, cols], gsib.at[:, :, cols], g_send.at[hh], g_recv.at[hh], sib
        )
        cp.start()
        gcopies.append(cp)

    tile = weights.shape[2] // NT_OUT
    wown.wait()
    mine = gated[core].reshape(NY * rows, feats)
    for t in range(NT_OUT):
        acc[t] = mm(mine, weights[core, :, t * tile : (t + 1) * tile])
    wsib.wait()
    for cp in gcopies:
        cp.wait()
    other = gsib[...].reshape(NY * rows, feats)
    y1, y2, y3 = [lax.rem(y + s, NY) for s in range(1, NY)]
    order = range(NT_OUT)
    for t in order:
        val = acc[t] + mm(other, weights[1 - core, :, t * tile : (t + 1) * tile])
        psend[t] = val.reshape(NY, rows, tile).astype(bf16)
        up = t % 2 == 0
        cp = remote(psend.at[t, y2], pvia.at[t], p_send.at[0, t], v_recv.at[t], ynext if up else yprev)
        cp.start()
        started.append(cp)
        cp = remote(
            psend.at[t, y3 if up else y1],
            precv.at[1 if up else 0, t],
            p_send.at[1, t],
            p_recv.at[1 if up else 0, t],
            yprev if up else ynext,
        )
        cp.start()
        started.append(cp)
    for t in order:
        up = t % 2 == 0
        near = y1 if up else y3
        remote(
            psend.at[t, 0], pvia.at[t], p_send.at[0, t], v_recv.at[t], yprev if up else ynext
        ).wait_recv()
        psend[t, near] = (psend[t, near].astype(f32) + pvia[t].astype(f32)).astype(bf16)
        cp = remote(
            psend.at[t, near],
            precv.at[0 if up else 1, t],
            p_send.at[2, t],
            p_recv.at[0 if up else 1, t],
            ynext if up else yprev,
        )
        cp.start()
        started.append(cp)
    for t in order:
        for side in range(2):
            remote(
                psend.at[t, 0],
                precv.at[side, t],
                p_send.at[0, t],
                p_recv.at[side, t],
                yprev if side == 0 else ynext,
            ).wait_recv()
        total = psend[t, y].astype(f32) + precv[0, t].astype(f32) + precv[1, t].astype(f32)
        out_ref[:, t * tile : (t + 1) * tile] = total.astype(bf16)

    @pl.when(x < NX - 1)
    def _():
        chain.wait_send()

    for cp in started:
        cp.wait_send()


def on_device(q, k, v, ld, wr, gate, gain, w):
    toks, feats = q.shape
    heads = feats // HS
    kd, width = w.shape
    rb = toks // (NY * NC)
    tile = width // NT_OUT
    anyspec = pl.BlockSpec(memory_space=pl.ANY)
    vmem, dma = pltpu.VMEM, pltpu.SemaphoreType.DMA
    return pl.pallas_call(
        kernel,
        in_specs=[anyspec] * 8,
        out_specs=pl.BlockSpec(memory_space=pltpu.VMEM),
        out_shape=jax.ShapeDtypeStruct((rb, width), bf16),
        scratch_shapes=[
            vmem((toks, feats), bf16),
            vmem((toks, feats), bf16),
            vmem((toks, feats), bf16),
            vmem((toks, feats), f32),
            vmem((heads, toks), f32),
            vmem((toks, feats), bf16),
            vmem((1, HS), f32),
            vmem((toks, feats), bf16),
            vmem((toks, feats), f32),
            vmem((NZ, MSG, HS), bf16),
            vmem((NZ, MSG, HS), bf16),
            vmem((NZ, HS + HALF, HS), f32),
            vmem((HALF, HS), bf16),
            vmem((HALF, HS), bf16),
            vmem((NZ, HALF, HS), bf16),
            vmem((NZ, HALF, HS), bf16),
            vmem((NC, NY, rb, kd), bf16),
            vmem((NY, rb, kd), bf16),
            vmem((NC, kd, width), bf16),
            vmem((NT_OUT, NY * rb, tile), f32),
            vmem((NT_OUT, NY, rb, tile), bf16),
            vmem((NT_OUT, rb, tile), bf16),
            vmem((2, NT_OUT, rb, tile), bf16),
            dma((7,)),
            dma((NZ,)),
            dma((NZ,)),
            dma,
            dma,
            dma((NZ,)),
            dma((NZ,)),
            dma((heads,)),
            dma((heads,)),
            dma,
            dma,
            dma,
            dma((3, NT_OUT)),
            dma((NT_OUT,)),
            dma((2, NT_OUT)),
        ],
        compiler_params=pltpu.CompilerParams(
            collective_id=0, has_side_effects=True, vmem_limit_bytes=56 << 20
        ),
        name="delta_layer",
    )(q, k, v, ld, wr.T, gate, gain.reshape(1, HS), w)


def solution(mesh):
    in_specs = (
        P("ctx", "head"),
        P("ctx", "head"),
        P("ctx", "head"),
        P("ctx", "head"),
        P("ctx", "head"),
        P("ctx", "head"),
        P(),
        P("head", None),
    )
    out_specs = P(("ctx", "head"), None)
    return jax.shard_map(
        on_device, mesh=mesh, in_specs=in_specs, out_specs=out_specs, check_vma=False
    )
```

time: 101 us -> 50 us (0.50)
  Pallas kernels: 93.1 us -> 48.2 us
  local copies, waits for them, and re-layouts: 7.42 us -> 1.64 us
    pallas_call x2 -> x1, Pallas kernels: 93.1 us -> 48.2 us  [on_device(): pl.pallas_call(kernel, in_specs=[anyspec] * 8, out_specs=pl.BlockSpec(mem...]
    unnamed x16 -> x1, local copies, waits for them, and re-layouts: 7.42 us -> 1.64 us
where the time goes in v2:
time: 50 us; the launch traced here: 49.9 us
  Pallas kernels  48.2 us (96%)
  local copies, waits for them, and re-layouts  1.64 us (3%)
    pallas_call x1, Pallas kernels, on_device(): pl.pallas_call(kernel, in_specs=[anyspec] * 8, out_specs=pl.BlockSpec(mem...  48.2 us
    unnamed x1, local copies, waits for them, and re-layouts  1.64 us

profile of v2, /device:TPU:6, one launch (start us, length us, event | category | flops | bytes accessed | tf_op | source)
XLA Modules:
  0.0 49.9 jit_solution(10079559391530844670)
XLA Ops:
  0.0 48.2 %delta_layer.1 = bf16[48,2304]{1,0:T(8,128)(2,1)} custom-call(bf16[384,512]{1,0:T(8,128)(2,1)} %q_hbm.1, bf16[384,512]{1,0:T(8,128)(2,1)} %k_hbm.1, bf16[384,512]{1,0:T(8,128)(2,1)} %v_hbm.1, f32[384,512]{1,0:T(8,128)} %ld_hbm.1, f32[4,384]{1,0:T(4,128)} %bitcast.2, bf16[384,512]{1,0:T(8,128)(2,1)} %gate_hbm.1, f32[1,128]{1,0:T(1,128)} %bitcast.3, ...), custom_call_target="tpu_custom_call" | custom-call | tf_op jit(solution)/shard_map/delta_layer/pallas_call | solution.py:368
  48.2 1.6 %copy.10 = bf16[48,2304]{1,0:T(8,128)(2,1)} copy(bf16[48,2304]{1,0:T(8,128)(2,1)} %delta_layer.1) | data formatting | bytes 442368

commit v3 on v2

--- a/solution.py
+++ b/solution.py
@@ -10,9 +10,9 @@
 W = 2 * C
 NX, NZ = 4, 8
 NY, NC = 4, 2
-MSG = 208
-HALF = HS // 2
-NT_OUT = 6
+MSG = 2 * HS + 16
+OWNER = (1, 5, 3, 7)
+NT_OUT = 9
 MESH = pl.DeviceIdType.MESH
 bf16, f32 = jnp.bfloat16, jnp.float32
 NN, NT, TN = ((1,), (0,)), ((1,), (1,)), ((0,), (0,))
@@ -127,9 +127,13 @@
     loc_ref,
     msg_ref,
     rmsg,
-    pre,
-    s0_out,
-    s0_in,
+    pre_map,
+    pre_state,
+    s_out,
+    s_in,
+    t_out,
+    t_in,
+    s0,
     sin_out,
     sin,
     gated,
@@ -159,9 +163,9 @@
     head = lax.axis_index("head")
     x, z = ctx // NZ, ctx % NZ
     y, core = head // NC, head % NC
-    feats = qd_ref.shape[1]
+    feats = qd_ref.shape[2]
     heads = feats // HS
-    rows = qd_ref.shape[0] // (NY * NC)
+    rows = qd_ref.shape[1] // NY
     sib = (ctx, y * NC + (1 - core))
 
     def zdev(zz):
@@ -169,10 +173,13 @@
 
     ynext = (ctx, lax.rem(y + 1, NY) * NC + core)
     yprev = (ctx, lax.rem(y + NY - 1, NY) * NC + core)
-    xnext = (lax.rem(x + 1, NX) * NZ + z, head)
-    xprev = (lax.rem(x + NX - 1, NX) * NZ + z, head)
+
+    def xdev(xx):
+        return (xx * NZ + z, head)
+
     barrier = pltpu.get_barrier_semaphore()
-    peers = [zdev(lax.rem(z + s, NZ)) for s in range(1, NZ)] + [ynext, yprev, sib, xnext, xprev]
+    peers = [zdev(lax.rem(z + s, NZ)) for s in range(1, NZ)] + [ynext, yprev, sib]
+    peers += [xdev(lax.rem(x + s, NX)) for s in range(1, NX)]
     for peer in peers:
         pl.semaphore_signal(barrier, inc=1, device_id=peer, device_id_type=MESH)
 
@@ -206,103 +213,136 @@
     for h in range(heads):
         cols = slice(h * HS, (h + 1) * HS)
         args.append((q_ref[:, cols], k_ref[:, cols], v_ref[:, cols], ld_ref[:, cols], beta[:, h : h + 1]))
-    ti = lax.broadcasted_iota(jnp.int32, (MSG - HS - HALF, HS), 0)
+    ti = lax.broadcasted_iota(jnp.int32, (MSG - 2 * HS, HS), 0)
     for h, (qd, loc, take, state, total) in enumerate(prep(args)):
         cols = slice(h * HS, (h + 1) * HS)
         for p in range(len(qd)):
-            qd_ref[p * W : (p + 1) * W, cols] = qd[p]
-            loc_ref[p * W : (p + 1) * W, cols] = loc[p]
+            lo = p * W
+            while lo < (p + 1) * W:
+                jj = lo // rows
+                hi = min((p + 1) * W, (jj + 1) * rows)
+                to = (jj // NC) * rows + lo - jj * rows
+                qd_ref[jj % NC, to : to + hi - lo, cols] = qd[p][lo - p * W : hi - p * W]
+                loc_ref[jj % NC, to : to + hi - lo, cols] = loc[p][lo - p * W : hi - p * W]
+                lo = hi
         t1 = total.astype(bf16).astype(f32)
         t2 = (total - t1).astype(bf16).astype(f32)
         t3 = total - t1 - t2
         tail = jnp.where(ti == 0, t1, jnp.where(ti == 1, t2, jnp.where(ti == 2, t3, 0.0)))
-        for c in range(2):
-            msg_ref[2 * h + c, :HS] = take.astype(bf16)
-            msg_ref[2 * h + c, HS : HS + HALF] = state[c * HALF : (c + 1) * HALF].astype(bf16)
-            msg_ref[2 * h + c, HS + HALF :] = tail.astype(bf16)
+        msg_ref[h, :HS] = take.astype(bf16)
+        msg_ref[h, HS : 2 * HS] = state.astype(bf16)
+        msg_ref[h, 2 * HS :] = tail.astype(bf16)
 
     pl.semaphore_wait(barrier, len(peers))
 
-    started = []
+    sends = []
+    for h in range(heads):
+        sends.append(remote(msg_ref.at[h], rmsg.at[z], m_send.at[h], m_recv.at[z], zdev(OWNER[h])))
+
+        @pl.when(z != OWNER[h])
+        def _(h=h):
+            sends[h].start()
+
+        @pl.when(z == OWNER[h])
+        def _(h=h):
+            rmsg[OWNER[h]] = msg_ref[h]
+
+    wsib = remote(w_hbm, weights.at[core], w_send, w_recv, sib)
+    wsib.start()
+
+    owner = z % 2 == 1
+    slot = (z - 1) // 4 + 2 * (((z - 1) // 2) % 2)
+    to1 = remote(s_out, s_in, x_send.at[0], x_recv.at[0], xdev(1))
+    to2 = remote(s_out, s_in, x_send.at[0], x_recv.at[0], xdev(2))
+    to3 = remote(s_out, s_in, x_send.at[1], x_recv.at[0], xdev(3))
+    tot3 = remote(t_out, t_in, x_send.at[0], x_recv.at[1], xdev(3))
+    backs = []
     for s in (4, 3, 5, 2, 6, 1, 7):
         zz = lax.rem(z + s, NZ)
-        cp = remote(msg_ref.at[zz], rmsg.at[z], m_send.at[s], m_recv.at[z], zdev(zz))
-        cp.start()
-        started.append(cp)
-    wsib = remote(w_hbm, weights.at[core], w_send, w_recv, sib)
-    wsib.start()
-    rmsg[z] = msg_ref[z]
-
-    ei = lax.broadcasted_iota(jnp.int32, (HS + HALF, HS), 0)
-    ej = lax.broadcasted_iota(jnp.int32, (HS + HALF, HS), 1)
-    run = (ei == ej).astype(f32)
-    for zz in range(NZ):
-
-        @pl.when(z != zz)
-        def _(zz=zz):
-            remote(msg_ref.at[0], rmsg.at[zz], m_send.at[0], m_recv.at[zz], zdev(zz)).wait_recv()
-
-        pre[zz] = run
-        d = jnp.sum(rmsg[zz, HS + HALF :, :].astype(f32), axis=0, keepdims=True)
-        new = run * d - mm(run, rmsg[zz, :HS, :])
-        run = jnp.concatenate([new[:HS], new[HS:] + rmsg[zz, HS : HS + HALF, :].astype(f32)], 0)
-
-    chain = remote(s0_out, s0_in, x_send, x_recv, xnext)
-
-    @pl.when(x == 0)
+        backs.append((zz, remote(sin_out.at[zz], sin.at[slot], s_send.at[s], s_recv.at[slot], zdev(zz))))
+
+    @pl.when(owner)
     def _():
-        s0_in[...] = jnp.zeros_like(s0_in)
-
-    @pl.when(x > 0)
-    def _():
-        remote(s0_out, s0_in, x_send, x_recv, xprev).wait_recv()
-
-    s0 = s0_in[...]
-
-    @pl.when(x < NX - 1)
-    def _():
-        s0_out[...] = (mm(s0, run[:HS]) + run[HS:]).astype(bf16)
-        chain.start()
-
-    for s in (4, 3, 5, 2, 6, 1, 7):
-        zz = lax.rem(z + s, NZ)
-        sin_out[zz] = (mm(s0, pre[zz, :HS, :]) + pre[zz, HS:, :]).astype(bf16)
-        cp = remote(sin_out.at[zz], sin.at[z], s_send.at[s], s_recv.at[z], zdev(zz))
-        cp.start()
-        started.append(cp)
-    sin[z] = (mm(s0, pre[z, :HS, :]) + pre[z, HS:, :]).astype(bf16)
+        ei = lax.broadcasted_iota(jnp.int32, (2 * HS, HS), 0)
+        ej = lax.broadcasted_iota(jnp.int32, (2 * HS, HS), 1)
+        run = (ei == ej).astype(f32)
+        for zz in range(NZ):
+
+            @pl.when(z != zz)
+            def _(zz=zz):
+                remote(msg_ref.at[0], rmsg.at[zz], m_send.at[0], m_recv.at[zz], zdev(zz)).wait_recv()
+
+            pre_map[zz] = run[:HS].astype(bf16)
+            pre_state[zz] = run[HS:]
+            d = jnp.sum(rmsg[zz, 2 * HS :, :].astype(f32), axis=0, keepdims=True)
+            new = run * d - mm(run, rmsg[zz, :HS, :])
+            run = jnp.concatenate([new[:HS], new[HS:] + rmsg[zz, HS : 2 * HS, :].astype(f32)], 0)
+
+        @pl.when(x == 0)
+        def _():
+            s_out[...] = run[HS:].astype(bf16)
+            to1.start()
+            s_in[...] = jnp.zeros_like(s_in)
+
+        @pl.when(x == 2)
+        def _():
+            t_out[...] = run.astype(bf16)
+            tot3.start()
+
+        @pl.when(x > 0)
+        def _():
+            to1.wait_recv()
+
+        @pl.when(x == 1)
+        def _():
+            s_out[...] = (mm(s_in[...], run[:HS]) + run[HS:]).astype(bf16)
+            to3.start()
+            to2.start()
+
+        @pl.when(x < 3)
+        def _():
+            s0[...] = s_in[...]
+
+        @pl.when(x == 3)
+        def _():
+            tot3.wait_recv()
+            s0[...] = (mm(s_in[...], t_in[:HS]) + t_in[HS:].astype(f32)).astype(bf16)
+
+        for zz, cp in backs:
+            sin_out[zz] = (mm(s0[...], pre_map[zz]) + pre_state[zz]).astype(bf16)
+            cp.start()
+        sin[slot] = (mm(s0[...], pre_map[z]) + pre_state[z]).astype(bf16)
+
+    for h in range(heads):
+
+        @pl.when(z != OWNER[h])
+        def _(h=h):
+            remote(sin_out.at[0], sin.at[h], s_send.at[0], s_recv.at[h], zdev(OWNER[h])).wait_recv()
 
     gcopies = []
-    for hh in range(heads):
-        for slot in (2 * hh, 2 * hh + 1):
-
-            @pl.when(z != slot)
-            def _(slot=slot):
-                remote(sin_out.at[0], sin.at[slot], s_send.at[0], s_recv.at[slot], zdev(slot)).wait_recv()
-
-        state = jnp.concatenate([sin[2 * hh], sin[2 * hh + 1]], 0)
-        cols = slice(hh * HS, (hh + 1) * HS)
-        att = mm(qd_ref[:, cols], state, NT) + loc_ref[:, cols]
-        ms = jnp.mean(att * att, axis=-1, keepdims=True)
-        gate = jax.nn.sigmoid(gate_ref[:, cols].astype(f32))
-        g = (att * lax.rsqrt(ms + 1e-5) * gain_ref[...] * gate).astype(bf16)
-        for jj in range(NY * NC):
-            gated[jj % NC, jj // NC, :, cols] = g[jj * rows : (jj + 1) * rows]
-        cp = remote(
-            gated.at[1 - core, :, :, cols], gsib.at[:, :, cols], g_send.at[hh], g_recv.at[hh], sib
-        )
-        cp.start()
-        gcopies.append(cp)
-
+    for part in (1 - core, core):
+        for h in range(heads):
+            cols = slice(h * HS, (h + 1) * HS)
+            att = mm(qd_ref[part, :, cols], sin[h], NT) + loc_ref[part, :, cols]
+            ms = jnp.mean(att * att, axis=-1, keepdims=True)
+            gate = jax.nn.sigmoid(gate_ref[:, part, :, cols].astype(f32).reshape(NY * rows, HS))
+            g = att * lax.rsqrt(ms + 1e-5) * gain_ref[...] * gate
+            gated[part, :, cols] = g.astype(bf16)
+            if len(gcopies) < heads:
+                cp = remote(gated.at[part, :, cols], gsib.at[:, cols], g_send.at[h], g_recv.at[h], sib)
+                cp.start()
+                gcopies.append(cp)
+
+    started = []
     tile = weights.shape[2] // NT_OUT
     wown.wait()
-    mine = gated[core].reshape(NY * rows, feats)
+    mine = gated[core]
     for t in range(NT_OUT):
         acc[t] = mm(mine, weights[core, :, t * tile : (t + 1) * tile])
     wsib.wait()
     for cp in gcopies:
         cp.wait()
-    other = gsib[...].reshape(NY * rows, feats)
+    other = gsib[...]
     y1, y2, y3 = [lax.rem(y + s, NY) for s in range(1, NY)]
     order = range(NT_OUT)
     for t in order:
@@ -349,9 +389,30 @@
         total = psend[t, y].astype(f32) + precv[0, t].astype(f32) + precv[1, t].astype(f32)
         out_ref[:, t * tile : (t + 1) * tile] = total.astype(bf16)
 
-    @pl.when(x < NX - 1)
+    for h in range(heads):
+
+        @pl.when(z != OWNER[h])
+        def _(h=h):
+            sends[h].wait_send()
+
+    @pl.when(owner)
     def _():
-        chain.wait_send()
+        for _, cp in backs:
+            cp.wait_send()
+
+    @pl.when(owner & (x < 3))
+    def _():
+        @pl.when(x == 2)
+        def _():
+            tot3.wait_send()
+
+        @pl.when(x < 2)
+        def _():
+            to1.wait_send()
+
+        @pl.when(x == 1)
+        def _():
+            to3.wait_send()
 
     for cp in started:
         cp.wait_send()
@@ -376,31 +437,35 @@
             vmem((toks, feats), bf16),
             vmem((toks, feats), f32),
             vmem((heads, toks), f32),
-            vmem((toks, feats), bf16),
+            vmem((NY, NC, rb, feats), bf16),
             vmem((1, HS), f32),
-            vmem((toks, feats), bf16),
-            vmem((toks, feats), f32),
+            vmem((NC, NY * rb, feats), bf16),
+            vmem((NC, NY * rb, feats), f32),
+            vmem((heads, MSG, HS), bf16),
             vmem((NZ, MSG, HS), bf16),
-            vmem((NZ, MSG, HS), bf16),
-            vmem((NZ, HS + HALF, HS), f32),
-            vmem((HALF, HS), bf16),
-            vmem((HALF, HS), bf16),
-            vmem((NZ, HALF, HS), bf16),
-            vmem((NZ, HALF, HS), bf16),
-            vmem((NC, NY, rb, kd), bf16),
-            vmem((NY, rb, kd), bf16),
+            vmem((NZ, HS, HS), bf16),
+            vmem((NZ, HS, HS), f32),
+            vmem((HS, HS), bf16),
+            vmem((HS, HS), bf16),
+            vmem((2 * HS, HS), bf16),
+            vmem((2 * HS, HS), bf16),
+            vmem((HS, HS), bf16),
+            vmem((NZ, HS, HS), bf16),
+            vmem((heads, HS, HS), bf16),
+            vmem((NC, NY * rb, kd), bf16),
+            vmem((NY * rb, kd), bf16),
             vmem((NC, kd, width), bf16),
             vmem((NT_OUT, NY * rb, tile), f32),
             vmem((NT_OUT, NY, rb, tile), bf16),
             vmem((NT_OUT, rb, tile), bf16),
             vmem((2, NT_OUT, rb, tile), bf16),
             dma((7,)),
+            dma((heads,)),
             dma((NZ,)),
+            dma((2,)),
+            dma((2,)),
             dma((NZ,)),
-            dma,
-            dma,
-            dma((NZ,)),
-            dma((NZ,)),
+            dma((heads,)),
             dma((heads,)),
             dma((heads,)),
             dma,
@@ -414,7 +479,7 @@
             collective_id=0, has_side_effects=True, vmem_limit_bytes=56 << 20
         ),
         name="delta_layer",
-    )(q, k, v, ld, wr.T, gate, gain.reshape(1, HS), w)
+    )(q, k, v, ld, wr.T, gate.reshape(NY, NC, rb, feats), gain.reshape(1, HS), w)
 
 
 def solution(mesh):

time: 50 us -> 50.4 us (level)
  no operation moved by 1% of the time
where the time goes in v3:
time: 50.4 us; the launch traced here: 50.3 us
  Pallas kernels  48.6 us (96%)
  local copies, waits for them, and re-layouts  1.64 us (3%)
    pallas_call x1, Pallas kernels, on_device(): pl.pallas_call(kernel, in_specs=[anyspec] * 8, out_specs=pl.BlockSpec(mem...  48.6 us
    unnamed x1, local copies, waits for them, and re-layouts  1.64 us

profile of v3, /device:TPU:6, one launch (start us, length us, event | category | flops | bytes accessed | tf_op | source)
XLA Modules:
  0.0 50.3 jit_solution(14257274880091982441)
XLA Ops:
  0.0 48.6 %delta_layer.1 = bf16[48,2304]{1,0:T(8,128)(2,1)} custom-call(bf16[384,512]{1,0:T(8,128)(2,1)} %q_hbm.1, bf16[384,512]{1,0:T(8,128)(2,1)} %k_hbm.1, bf16[384,512]{1,0:T(8,128)(2,1)} %v_hbm.1, f32[384,512]{1,0:T(8,128)} %ld_hbm.1, f32[4,384]{1,0:T(4,128)} %bitcast.4, bf16[4,2,48,512]{3,2,1,0:T(8,128)(2,1)} %bitcast.3, f32[1,128]{1,0:T(1,128)} %bitcast.5, ...), custom_call_target="tpu_custom_call" | custom-call | tf_op jit(solution)/shard_map/delta_layer/pallas_call | solution.py:429
  48.7 1.6 %copy.10 = bf16[48,2304]{1,0:T(8,128)(2,1)} copy(bf16[48,2304]{1,0:T(8,128)(2,1)} %delta_layer.1) | data formatting | bytes 442368

commit v4 on v3

--- a/solution.py
+++ b/solution.py
@@ -12,7 +12,7 @@
 NY, NC = 4, 2
 MSG = 2 * HS + 16
 OWNER = (1, 5, 3, 7)
-NT_OUT = 9
+NT_OUT = 6
 MESH = pl.DeviceIdType.MESH
 bf16, f32 = jnp.bfloat16, jnp.float32
 NN, NT, TN = ((1,), (0,)), ((1,), (1,)), ((0,), (0,))
@@ -252,10 +252,9 @@
 
     owner = z % 2 == 1
     slot = (z - 1) // 4 + 2 * (((z - 1) // 2) % 2)
-    to1 = remote(s_out, s_in, x_send.at[0], x_recv.at[0], xdev(1))
-    to2 = remote(s_out, s_in, x_send.at[0], x_recv.at[0], xdev(2))
-    to3 = remote(s_out, s_in, x_send.at[1], x_recv.at[0], xdev(3))
-    tot3 = remote(t_out, t_in, x_send.at[0], x_recv.at[1], xdev(3))
+    states = [remote(s_out, s_in, x_send.at[xx - 1], x_recv.at[0], xdev(xx)) for xx in (3, 2, 1)]
+    totals1 = [remote(t_out, t_in.at[0], x_send.at[xx - 1], x_recv.at[1], xdev(xx)) for xx in (3, 2)]
+    totals2 = [remote(t_out, t_in.at[1], x_send.at[xx - 1], x_recv.at[2], xdev(xx)) for xx in (3,)]
     backs = []
     for s in (4, 3, 5, 2, 6, 1, 7):
         zz = lax.rem(z + s, NZ)
@@ -281,110 +280,130 @@
         @pl.when(x == 0)
         def _():
             s_out[...] = run[HS:].astype(bf16)
-            to1.start()
-            s_in[...] = jnp.zeros_like(s_in)
+            for cp in states:
+                cp.start()
+            s0[...] = jnp.zeros_like(s0)
+
+        @pl.when((x == 1) | (x == 2))
+        def _():
+            t_out[...] = run.astype(bf16)
+
+        @pl.when(x == 1)
+        def _():
+            for cp in totals1:
+                cp.start()
+            states[0].wait_recv()
+            s0[...] = s_in[...]
 
         @pl.when(x == 2)
         def _():
-            t_out[...] = run.astype(bf16)
-            tot3.start()
-
-        @pl.when(x > 0)
+            totals2[0].start()
+
+        @pl.when(x >= 2)
         def _():
-            to1.wait_recv()
-
-        @pl.when(x == 1)
-        def _():
-            s_out[...] = (mm(s_in[...], run[:HS]) + run[HS:]).astype(bf16)
-            to3.start()
-            to2.start()
-
-        @pl.when(x < 3)
-        def _():
-            s0[...] = s_in[...]
+            states[0].wait_recv()
+            totals1[0].wait_recv()
+            s0[...] = (mm(s_in[...], t_in[0, :HS]) + t_in[0, HS:].astype(f32)).astype(bf16)
 
         @pl.when(x == 3)
         def _():
-            tot3.wait_recv()
-            s0[...] = (mm(s_in[...], t_in[:HS]) + t_in[HS:].astype(f32)).astype(bf16)
-
+            totals2[0].wait_recv()
+            s0[...] = (mm(s0[...], t_in[1, :HS]) + t_in[1, HS:].astype(f32)).astype(bf16)
+
+        s0v = s0[...]
+        for zz in range(NZ):
+            sin_out[zz] = (mm(s0v, pre_map[zz]) + pre_state[zz]).astype(bf16)
         for zz, cp in backs:
-            sin_out[zz] = (mm(s0[...], pre_map[zz]) + pre_state[zz]).astype(bf16)
             cp.start()
-        sin[slot] = (mm(s0[...], pre_map[z]) + pre_state[z]).astype(bf16)
-
+        sin[slot] = sin_out[z]
+
+    def read(part, h):
+        cols = slice(h * HS, (h + 1) * HS)
+        att = mm(qd_ref[part, :, cols], sin[h], NT) + loc_ref[part, :, cols]
+        ms = jnp.mean(att * att, axis=-1, keepdims=True)
+        gate = jax.nn.sigmoid(gate_ref[:, part, :, cols].astype(f32).reshape(NY * rows, HS))
+        return (att * lax.rsqrt(ms + 1e-5) * gain_ref[...] * gate).astype(bf16)
+
+    gcopies = []
+    for pair in range(heads // 2):
+        two = (2 * pair, 2 * pair + 1)
+        for h in two:
+
+            @pl.when(z != OWNER[h])
+            def _(h=h):
+                remote(sin_out.at[0], sin.at[h], s_send.at[0], s_recv.at[h], zdev(OWNER[h])).wait_recv()
+
+        out = [read(1 - core, h) for h in two]
+        cols = slice(two[0] * HS, (two[1] + 1) * HS)
+        gated[1 - core, :, cols] = jnp.concatenate(out, 1)
+        cp = remote(gated.at[1 - core, :, cols], gsib.at[:, cols], g_send.at[pair], g_recv.at[pair], sib)
+        cp.start()
+        gcopies.append(cp)
     for h in range(heads):
-
-        @pl.when(z != OWNER[h])
-        def _(h=h):
-            remote(sin_out.at[0], sin.at[h], s_send.at[0], s_recv.at[h], zdev(OWNER[h])).wait_recv()
-
-    gcopies = []
-    for part in (1 - core, core):
-        for h in range(heads):
-            cols = slice(h * HS, (h + 1) * HS)
-            att = mm(qd_ref[part, :, cols], sin[h], NT) + loc_ref[part, :, cols]
-            ms = jnp.mean(att * att, axis=-1, keepdims=True)
-            gate = jax.nn.sigmoid(gate_ref[:, part, :, cols].astype(f32).reshape(NY * rows, HS))
-            g = att * lax.rsqrt(ms + 1e-5) * gain_ref[...] * gate
-            gated[part, :, cols] = g.astype(bf16)
-            if len(gcopies) < heads:
-                cp = remote(gated.at[part, :, cols], gsib.at[:, cols], g_send.at[h], g_recv.at[h], sib)
-                cp.start()
-                gcopies.append(cp)
+        gated[core, :, h * HS : (h + 1) * HS] = read(core, h)
 
     started = []
     tile = weights.shape[2] // NT_OUT
+    wide = 2 * tile
     wown.wait()
     mine = gated[core]
-    for t in range(NT_OUT):
-        acc[t] = mm(mine, weights[core, :, t * tile : (t + 1) * tile])
+    for t in range(NT_OUT // 2):
+        acc[t] = mm(mine, weights[core, :, t * wide : (t + 1) * wide])
     wsib.wait()
     for cp in gcopies:
         cp.wait()
     other = gsib[...]
     y1, y2, y3 = [lax.rem(y + s, NY) for s in range(1, NY)]
-    order = range(NT_OUT)
-    for t in order:
-        val = acc[t] + mm(other, weights[1 - core, :, t * tile : (t + 1) * tile])
-        psend[t] = val.reshape(NY, rows, tile).astype(bf16)
-        up = t % 2 == 0
-        cp = remote(psend.at[t, y2], pvia.at[t], p_send.at[0, t], v_recv.at[t], ynext if up else yprev)
-        cp.start()
-        started.append(cp)
+    for t in range(NT_OUT // 2):
+        val = acc[t] + mm(other, weights[1 - core, :, t * wide : (t + 1) * wide])
+        val = val.reshape(NY, rows, wide).astype(bf16)
+        for u in range(2):
+            psend[2 * t + u] = val[:, :, u * tile : (u + 1) * tile]
+        for u in range(2):
+            n = 2 * t + u
+            cp = remote(psend.at[n, y2], pvia.at[n], p_send.at[0, n], v_recv.at[n], (ynext, yprev)[u])
+            cp.start()
+            started.append(cp)
+    for t in range(NT_OUT):
+        u = t % 2
         cp = remote(
-            psend.at[t, y3 if up else y1],
-            precv.at[1 if up else 0, t],
+            psend.at[t, (y3, y1)[u]],
+            precv.at[1 - u, t],
             p_send.at[1, t],
-            p_recv.at[1 if up else 0, t],
-            yprev if up else ynext,
+            p_recv.at[1 - u, t],
+            (yprev, ynext)[u],
         )
         cp.start()
         started.append(cp)
-    for t in order:
-        up = t % 2 == 0
-        near = y1 if up else y3
-        remote(
-            psend.at[t, 0], pvia.at[t], p_send.at[0, t], v_recv.at[t], yprev if up else ynext
-        ).wait_recv()
-        psend[t, near] = (psend[t, near].astype(f32) + pvia[t].astype(f32)).astype(bf16)
-        cp = remote(
-            psend.at[t, near],
-            precv.at[0 if up else 1, t],
-            p_send.at[2, t],
-            p_recv.at[0 if up else 1, t],
-            ynext if up else yprev,
-        )
-        cp.start()
-        started.append(cp)
-    for t in order:
+    for t in range(NT_OUT // 2):
+        for u in range(2):
+            n = 2 * t + u
+            remote(
+                psend.at[n, 0], pvia.at[n], p_send.at[0, n], v_recv.at[n], (yprev, ynext)[u]
+            ).wait_recv()
+        for u in range(2):
+            n = 2 * t + u
+            near = (y1, y3)[u]
+            psend[n, near] = (psend[n, near].astype(f32) + pvia[n].astype(f32)).astype(bf16)
+        for u in range(2):
+            n = 2 * t + u
+            cp = remote(
+                psend.at[n, (y1, y3)[u]],
+                precv.at[u, n],
+                p_send.at[2, n],
+                p_recv.at[u, n],
+                (ynext, yprev)[u],
+            )
+            cp.start()
+            started.append(cp)
+    for t in range(NT_OUT):
         for side in range(2):
             remote(
                 psend.at[t, 0],
                 precv.at[side, t],
                 p_send.at[0, t],
                 p_recv.at[side, t],
-                yprev if side == 0 else ynext,
+                (yprev, ynext)[side],
             ).wait_recv()
         total = psend[t, y].astype(f32) + precv[0, t].astype(f32) + precv[1, t].astype(f32)
         out_ref[:, t * tile : (t + 1) * tile] = total.astype(bf16)
@@ -400,19 +419,12 @@
         for _, cp in backs:
             cp.wait_send()
 
-    @pl.when(owner & (x < 3))
-    def _():
-        @pl.when(x == 2)
-        def _():
-            tot3.wait_send()
-
-        @pl.when(x < 2)
-        def _():
-            to1.wait_send()
-
-        @pl.when(x == 1)
-        def _():
-            to3.wait_send()
+    for xx, copies in enumerate((states, totals1, totals2)):
+
+        @pl.when(owner & (x == xx))
+        def _(copies=copies):
+            for cp in copies:
+                cp.wait_send()
 
     for cp in started:
         cp.wait_send()
@@ -448,22 +460,22 @@
             vmem((HS, HS), bf16),
             vmem((HS, HS), bf16),
             vmem((2 * HS, HS), bf16),
-            vmem((2 * HS, HS), bf16),
+            vmem((2, 2 * HS, HS), bf16),
             vmem((HS, HS), bf16),
             vmem((NZ, HS, HS), bf16),
             vmem((heads, HS, HS), bf16),
             vmem((NC, NY * rb, kd), bf16),
             vmem((NY * rb, kd), bf16),
             vmem((NC, kd, width), bf16),
-            vmem((NT_OUT, NY * rb, tile), f32),
+            vmem((NT_OUT // 2, NY * rb, 2 * tile), f32),
             vmem((NT_OUT, NY, rb, tile), bf16),
             vmem((NT_OUT, rb, tile), bf16),
             vmem((2, NT_OUT, rb, tile), bf16),
             dma((7,)),
             dma((heads,)),
             dma((NZ,)),
-            dma((2,)),
-            dma((2,)),
+            dma((3,)),
+            dma((3,)),
             dma((NZ,)),
             dma((heads,)),
             dma((heads,)),

time: 50.4 us -> 46.5 us (0.923)
  Pallas kernels: 48.6 us -> 44.8 us
    pallas_call x1, Pallas kernels: 48.6 us -> 44.8 us  [on_device(): pl.pallas_call(kernel, in_specs=[anyspec] * 8, out_specs=pl.BlockSpec(mem...]
where the time goes in v4:
time: 46.5 us; the launch traced here: 46.4 us
  Pallas kernels  44.8 us (96%)
  local copies, waits for them, and re-layouts  1.64 us (4%)
    pallas_call x1, Pallas kernels, on_device(): pl.pallas_call(kernel, in_specs=[anyspec] * 8, out_specs=pl.BlockSpec(mem...  44.8 us
    unnamed x1, local copies, waits for them, and re-layouts  1.64 us

profile of v4, /device:TPU:6, one launch (start us, length us, event | category | flops | bytes accessed | tf_op | source)
XLA Modules:
  0.0 46.4 jit_solution(6807954166970543771)
XLA Ops:
  0.0 44.8 %delta_layer.1 = bf16[48,2304]{1,0:T(8,128)(2,1)} custom-call(bf16[384,512]{1,0:T(8,128)(2,1)} %q_hbm.1, bf16[384,512]{1,0:T(8,128)(2,1)} %k_hbm.1, bf16[384,512]{1,0:T(8,128)(2,1)} %v_hbm.1, f32[384,512]{1,0:T(8,128)} %ld_hbm.1, f32[4,384]{1,0:T(4,128)} %bitcast.4, bf16[4,2,48,512]{3,2,1,0:T(8,128)(2,1)} %bitcast.3, f32[1,128]{1,0:T(1,128)} %bitcast.5, ...), custom_call_target="tpu_custom_call" | custom-call | tf_op jit(solution)/shard_map/delta_layer/pallas_call | solution.py:441
  44.8 1.6 %copy.10 = bf16[48,2304]{1,0:T(8,128)(2,1)} copy(bf16[48,2304]{1,0:T(8,128)(2,1)} %delta_layer.1) | data formatting | bytes 442368

commit v5 on v4

--- a/solution.py
+++ b/solution.py
@@ -11,7 +11,7 @@
 NX, NZ = 4, 8
 NY, NC = 4, 2
 MSG = 2 * HS + 16
-OWNER = (1, 5, 3, 7)
+OWNER = (0, 4, 2, 6)
 NT_OUT = 6
 MESH = pl.DeviceIdType.MESH
 bf16, f32 = jnp.bfloat16, jnp.float32
@@ -24,46 +24,43 @@
     )
 
 
-def prep(heads):
+def masks():
     i = lax.broadcasted_iota(jnp.int32, (W, W), 0)
     j = lax.broadcasted_iota(jnp.int32, (W, W), 1)
+    return i, j
+
+
+def prep_maps(n_heads, n_blocks, read):
+    i, j = masks()
     lower = ((i >= j) & ((i // C) == (j // C))).astype(bf16)
     eye = (i == j).astype(f32)
     zero = jnp.zeros((W, W), bf16)
-    blocks = []
-    for q, k, v, ld, beta in heads:
-        n = q.shape[0] // W
-        for p in range(n):
-            s = slice(p * W, (p + 1) * W)
-            blocks.append(dict(q=q[s], k=k[s], v=v[s], ld=ld[s], beta=beta[s]))
-    for b in blocks:
-        hi = b["ld"].astype(bf16)
-        lo = (b["ld"] - hi.astype(f32)).astype(bf16)
+    blocks = [dict(h=h, p=p) for h in range(n_heads) for p in range(n_blocks)]
+    for b in blocks:
+        ld = read("ld", b)
+        hi = ld.astype(bf16)
+        lo = (ld - hi.astype(f32)).astype(bf16)
         b["cum"] = mm(lower, hi) + mm(lower, lo)
     for b in blocks:
-        kf = b["k"].astype(f32)
+        kf = read("k", b).astype(f32)
         unit = kf * lax.rsqrt(jnp.sum(kf * kf, axis=-1, keepdims=True) + 1e-6)
         cum = b.pop("cum")
+        b["beta"] = read("beta", b)
         e1, e2 = cum[C - 1 : C], cum[W - 1 : W]
         d1, d2 = jnp.exp(e1), jnp.exp(e2)
         grow = jnp.exp(cum)
         back = (unit * jnp.exp(-cum)).astype(bf16)
         kn = b["beta"] * (unit * grow)
-        qn = b["q"].astype(f32) * grow
         ke1 = unit[:C] * jnp.exp(e1 - cum[:C])
         ke2 = unit[C:] * jnp.exp(e2 - cum[C:])
-        knb, qnb = kn.astype(bf16), qn.astype(bf16)
-        top = mm(jnp.concatenate([knb[:C], qnb[:C]], 0), back, NT)
+        knb = kn.astype(bf16)
         earlier = jnp.concatenate([ke1.astype(bf16), back[C:]], 0)
-        bot = mm(jnp.concatenate([knb[C:], qnb[C:]], 0), earlier, NT)
-        b["a"] = jnp.where(i > j, jnp.concatenate([top[:C], bot[:C]], 0), 0.0).astype(bf16)
-        b["r"] = jnp.where(i >= j, jnp.concatenate([top[C:], bot[C:]], 0), 0.0).astype(bf16)
-        b["qn"] = jnp.concatenate([qn[:C], qn[C:] * d1], 0)
-        left = jnp.concatenate([knb[:C], (kn[C:] * d1).astype(bf16)], 0)
-        right = (b["beta"] * b["v"].astype(f32)).astype(bf16)
-        b["rhs"] = jnp.concatenate([left, right], 1)
+        a = jnp.concatenate([mm(knb[:C], back, NT), mm(knb[C:], earlier, NT)], 0)
+        b["a"] = jnp.where(i > j, a, 0.0).astype(bf16)
+        b["left"] = jnp.concatenate([knb[:C], (kn[C:] * d1).astype(bf16)], 0)
         b["ke"] = jnp.concatenate([(ke1 * d2).astype(bf16), ke2.astype(bf16)], 0)
         b["d"] = d1 * d2
+        b["later"] = (grow, d1, back, earlier)
     size = 1
     while size < W:
         mask = ((i // size) % 2 == 1) & ((j // size) == (i // size) - 1)
@@ -74,36 +71,44 @@
             b["t"] = eye - b["st"].astype(f32) if size == 1 else b["t"] - mm(b["t"], b["st"])
         size *= 2
     for b in blocks:
-        b["y"] = mm(b["t"], b["rhs"]).astype(bf16)
-    for b in blocks:
-        b["ry"] = mm(b["r"], b["y"])
+        right = (b["beta"] * read("v", b).astype(f32)).astype(bf16)
+        b["y"] = mm(b["t"], jnp.concatenate([b["left"], right], 1)).astype(bf16)
     for b in blocks:
         b["yk"] = mm(b["y"], b["ke"], TN)
-    n = len(blocks) // len(heads)
-    x = [None for _ in heads]
-    total = [None for _ in heads]
-    qd = [[] for _ in heads]
-    loc = [[] for _ in heads]
-    for p in range(n):
-        for h in range(len(heads)):
-            b = blocks[h * n + p]
-            qe = b["qn"] - b["ry"][:, :HS]
+    x = [None] * n_heads
+    total = [None] * n_heads
+    for p in range(n_blocks):
+        for h in range(n_heads):
+            b = blocks[h * n_blocks + p]
             if p == 0:
-                qd[h].append(qe.astype(bf16))
-                loc[h].append(b["ry"][:, HS:])
                 x[h] = jnp.concatenate([eye * b["d"] - b["yk"][:HS], b["yk"][HS:]], 0)
                 total[h] = b["d"]
             else:
-                xb = x[h].astype(bf16)
-                o = mm(qe, xb, NT)
-                qd[h].append(o[:, :HS].astype(bf16))
-                loc[h].append(o[:, HS:] + b["ry"][:, HS:])
-                nx = x[h] * b["d"] - mm(xb, b["yk"][:HS])
+                b["x"] = x[h].astype(bf16)
+                nx = x[h] * b["d"] - mm(b["x"], b["yk"][:HS])
                 x[h] = jnp.concatenate([nx[:HS], nx[HS:] + b["yk"][HS:]], 0)
                 total[h] = total[h] * b["d"]
-    return [
-        (qd[h], loc[h], eye * total[h] - x[h][:HS], x[h][HS:], total[h]) for h in range(len(heads))
-    ]
+    ends = [(eye * total[h] - x[h][:HS], x[h][HS:], total[h]) for h in range(n_heads)]
+    return blocks, ends
+
+
+def prep_reads(blocks, read, write):
+    i, j = masks()
+    for b in blocks:
+        grow, d1, back, earlier = b["later"]
+        qn = read("q", b).astype(f32) * grow
+        qnb = qn.astype(bf16)
+        r = jnp.concatenate([mm(qnb[:C], back, NT), mm(qnb[C:], earlier, NT)], 0)
+        b["r"] = jnp.where(i >= j, r, 0.0).astype(bf16)
+        b["qn"] = jnp.concatenate([qn[:C], qn[C:] * d1], 0)
+    for b in blocks:
+        b["ry"] = mm(b["r"], b["y"])
+    for b in blocks:
+        qe, local = b["qn"] - b["ry"][:, :HS], b["ry"][:, HS:]
+        if "x" in b:
+            o = mm(qe, b["x"], NT)
+            qe, local = o[:, :HS], o[:, HS:] + local
+        write(b, qe.astype(bf16), local)
 
 
 def kernel(
@@ -115,7 +120,9 @@
     gate_hbm,
     gain_hbm,
     w_hbm,
-    out_ref,
+    own_hbm,
+    prev_hbm,
+    next_hbm,
     q_ref,
     k_ref,
     v_ref,
@@ -142,7 +149,6 @@
     acc,
     psend,
     pvia,
-    precv,
     in_sem,
     m_send,
     m_recv,
@@ -158,7 +164,9 @@
     p_send,
     v_recv,
     p_recv,
+    o_sem,
 ):
+    outs = (prev_hbm, next_hbm)
     ctx = lax.axis_index("ctx")
     head = lax.axis_index("head")
     x, z = ctx // NZ, ctx % NZ
@@ -189,8 +197,8 @@
             (ld_hbm, ld_ref),
             (k_hbm, k_ref),
             (wr_hbm, wr_ref),
+            (v_hbm, v_ref),
             (q_hbm, q_ref),
-            (v_hbm, v_ref),
             (gate_hbm, gate_ref),
             (gain_hbm, gain_ref),
         )
@@ -200,31 +208,30 @@
         loads.append(cp)
     wown = pltpu.make_async_copy(w_hbm, weights.at[core], w_sem)
     wown.start()
-    for cp in loads:
-        cp.wait()
 
     def remote(src, dst, send, recv, dev):
         return pltpu.make_async_remote_copy(
             src_ref=src, dst_ref=dst, send_sem=send, recv_sem=recv, device_id=dev, device_id_type=MESH
         )
 
-    beta = wr_ref[...].T
-    args = []
-    for h in range(heads):
-        cols = slice(h * HS, (h + 1) * HS)
-        args.append((q_ref[:, cols], k_ref[:, cols], v_ref[:, cols], ld_ref[:, cols], beta[:, h : h + 1]))
+    waited = set()
+
+    def read(name, b):
+        for n in dict(ld=(0,), k=(1,), beta=(2,), v=(3,), q=(4,))[name]:
+            if n not in waited:
+                waited.add(n)
+                loads[n].wait()
+        at = (slice(b["p"] * W, (b["p"] + 1) * W), slice(b["h"] * HS, (b["h"] + 1) * HS))
+        if name == "beta":
+            if "beta" not in cache:
+                cache["beta"] = wr_ref[...].T
+            return cache["beta"][at[0], b["h"] : b["h"] + 1]
+        return dict(ld=ld_ref, k=k_ref, v=v_ref, q=q_ref)[name][at]
+
+    cache = {}
     ti = lax.broadcasted_iota(jnp.int32, (MSG - 2 * HS, HS), 0)
-    for h, (qd, loc, take, state, total) in enumerate(prep(args)):
-        cols = slice(h * HS, (h + 1) * HS)
-        for p in range(len(qd)):
-            lo = p * W
-            while lo < (p + 1) * W:
-                jj = lo // rows
-                hi = min((p + 1) * W, (jj + 1) * rows)
-                to = (jj // NC) * rows + lo - jj * rows
-                qd_ref[jj % NC, to : to + hi - lo, cols] = qd[p][lo - p * W : hi - p * W]
-                loc_ref[jj % NC, to : to + hi - lo, cols] = loc[p][lo - p * W : hi - p * W]
-                lo = hi
+    blocks, ends = prep_maps(heads, q_ref.shape[0] // W, read)
+    for h, (take, state, total) in enumerate(ends):
         t1 = total.astype(bf16).astype(f32)
         t2 = (total - t1).astype(bf16).astype(f32)
         t3 = total - t1 - t2
@@ -237,21 +244,36 @@
 
     sends = []
     for h in range(heads):
-        sends.append(remote(msg_ref.at[h], rmsg.at[z], m_send.at[h], m_recv.at[z], zdev(OWNER[h])))
-
-        @pl.when(z != OWNER[h])
+        sends.append(remote(msg_ref.at[h], rmsg.at[z], m_send.at[h], m_recv.at[z], zdev(OWNER[h] + core)))
+
+        @pl.when(z != OWNER[h] + core)
         def _(h=h):
             sends[h].start()
 
-        @pl.when(z == OWNER[h])
+        @pl.when(z == OWNER[h] + core)
         def _(h=h):
-            rmsg[OWNER[h]] = msg_ref[h]
+            rmsg[z] = msg_ref[h]
 
     wsib = remote(w_hbm, weights.at[core], w_send, w_recv, sib)
     wsib.start()
 
-    owner = z % 2 == 1
-    slot = (z - 1) // 4 + 2 * (((z - 1) // 2) % 2)
+    owner = z % 2 == core
+    slot = (z // 4) + 2 * ((z // 2) % 2)
+
+    def write(b, qd, local):
+        cols = slice(b["h"] * HS, (b["h"] + 1) * HS)
+        lo = b["p"] * W
+        while lo < (b["p"] + 1) * W:
+            jj = lo // rows
+            hi = min((b["p"] + 1) * W, (jj + 1) * rows)
+            to = (jj // NC) * rows + lo - jj * rows
+            qd_ref[jj % NC, to : to + hi - lo, cols] = qd[lo - b["p"] * W : hi - b["p"] * W]
+            loc_ref[jj % NC, to : to + hi - lo, cols] = local[lo - b["p"] * W : hi - b["p"] * W]
+            lo = hi
+
+    prep_reads(blocks, read, write)
+    for n in (5, 6):
+        loads[n].wait()
     states = [remote(s_out, s_in, x_send.at[xx - 1], x_recv.at[0], xdev(xx)) for xx in (3, 2, 1)]
     totals1 = [remote(t_out, t_in.at[0], x_send.at[xx - 1], x_recv.at[1], xdev(xx)) for xx in (3, 2)]
     totals2 = [remote(t_out, t_in.at[1], x_send.at[xx - 1], x_recv.at[2], xdev(xx)) for xx in (3,)]
@@ -329,9 +351,9 @@
         two = (2 * pair, 2 * pair + 1)
         for h in two:
 
-            @pl.when(z != OWNER[h])
+            @pl.when(z != OWNER[h] + core)
             def _(h=h):
-                remote(sin_out.at[0], sin.at[h], s_send.at[0], s_recv.at[h], zdev(OWNER[h])).wait_recv()
+                remote(sin_out.at[0], sin.at[h], s_send.at[0], s_recv.at[h], zdev(OWNER[h] + core)).wait_recv()
 
         out = [read(1 - core, h) for h in two]
         cols = slice(two[0] * HS, (two[1] + 1) * HS)
@@ -368,13 +390,18 @@
         u = t % 2
         cp = remote(
             psend.at[t, (y3, y1)[u]],
-            precv.at[1 - u, t],
+            outs[1 - u].at[:, t * tile : (t + 1) * tile],
             p_send.at[1, t],
             p_recv.at[1 - u, t],
             (yprev, ynext)[u],
         )
         cp.start()
         started.append(cp)
+    locals_ = []
+    for t in range(NT_OUT):
+        cp = pltpu.make_async_copy(psend.at[t, y], own_hbm.at[:, t * tile : (t + 1) * tile], o_sem.at[t])
+        cp.start()
+        locals_.append(cp)
     for t in range(NT_OUT // 2):
         for u in range(2):
             n = 2 * t + u
@@ -389,7 +416,7 @@
             n = 2 * t + u
             cp = remote(
                 psend.at[n, (y1, y3)[u]],
-                precv.at[u, n],
+                outs[u].at[:, n * tile : (n + 1) * tile],
                 p_send.at[2, n],
                 p_recv.at[u, n],
                 (ynext, yprev)[u],
@@ -398,19 +425,16 @@
             started.append(cp)
     for t in range(NT_OUT):
         for side in range(2):
+            cols = slice(t * tile, (t + 1) * tile)
             remote(
-                psend.at[t, 0],
-                precv.at[side, t],
-                p_send.at[0, t],
-                p_recv.at[side, t],
-                (yprev, ynext)[side],
+                psend.at[t, 0], outs[side].at[:, cols], p_send.at[0, t], p_recv.at[side, t], (yprev, ynext)[side]
             ).wait_recv()
-        total = psend[t, y].astype(f32) + precv[0, t].astype(f32) + precv[1, t].astype(f32)
-        out_ref[:, t * tile : (t + 1) * tile] = total.astype(bf16)
+    for cp in locals_:
+        cp.wait()
 
     for h in range(heads):
 
-        @pl.when(z != OWNER[h])
+        @pl.when(z != OWNER[h] + core)
         def _(h=h):
             sends[h].wait_send()
 
@@ -438,11 +462,12 @@
     tile = width // NT_OUT
     anyspec = pl.BlockSpec(memory_space=pl.ANY)
     vmem, dma = pltpu.VMEM, pltpu.SemaphoreType.DMA
-    return pl.pallas_call(
+    out = jax.ShapeDtypeStruct((rb, width), bf16)
+    own, one, two = pl.pallas_call(
         kernel,
         in_specs=[anyspec] * 8,
-        out_specs=pl.BlockSpec(memory_space=pltpu.VMEM),
-        out_shape=jax.ShapeDtypeStruct((rb, width), bf16),
+        out_specs=[anyspec] * 3,
+        out_shape=[out] * 3,
         scratch_shapes=[
             vmem((toks, feats), bf16),
             vmem((toks, feats), bf16),
@@ -470,7 +495,6 @@
             vmem((NT_OUT // 2, NY * rb, 2 * tile), f32),
             vmem((NT_OUT, NY, rb, tile), bf16),
             vmem((NT_OUT, rb, tile), bf16),
-            vmem((2, NT_OUT, rb, tile), bf16),
             dma((7,)),
             dma((heads,)),
             dma((NZ,)),
@@ -486,12 +510,14 @@
             dma((3, NT_OUT)),
             dma((NT_OUT,)),
             dma((2, NT_OUT)),
+            dma((NT_OUT,)),
         ],
         compiler_params=pltpu.CompilerParams(
             collective_id=0, has_side_effects=True, vmem_limit_bytes=56 << 20
         ),
         name="delta_layer",
     )(q, k, v, ld, wr.T, gate.reshape(NY, NC, rb, feats), gain.reshape(1, HS), w)
+    return (own.astype(f32) + one.astype(f32) + two.astype(f32)).astype(bf16)
 
 
 def solution(mesh):

time: 46.5 us -> 43.1 us (0.927)
  Pallas kernels: 44.8 us -> 41.1 us
  other arithmetic: 0 us -> 1.92 us
  local copies, waits for them, and re-layouts: 1.64 us -> 0 us
    pallas_call x1, Pallas kernels: 44.8 us -> 41.1 us  [on_device(): pl.pallas_call(kernel, in_specs=[anyspec] * 8, out_specs=[anyspec] * 3, o...]
    convert_element_type x0 -> x1, other arithmetic: none -> 1.92 us  [on_device(): return (own.astype(f32) + one.astype(f32) + two.astype(f32)).astype(bf16)]
    unnamed x1 -> x0, local copies, waits for them, and re-layouts: 1.64 us -> none
where the time goes in v5:
time: 43.1 us; the launch traced here: 43 us
  Pallas kernels  41.1 us (95%)
  other arithmetic  1.92 us (4%)
    pallas_call x1, Pallas kernels, on_device(): pl.pallas_call(kernel, in_specs=[anyspec] * 8, out_specs=[anyspec] * 3, o...  41.1 us
    convert_element_type x1, other arithmetic, on_device(): return (own.astype(f32) + one.astype(f32) + two.astype(f32)).astype(bf16)  1.92 us

profile of v5, /device:TPU:6, one launch (start us, length us, event | category | flops | bytes accessed | tf_op | source)
XLA Modules:
  0.0 43.0 jit_solution(17055751072439363960)
XLA Ops:
  0.0 41.1 %delta_layer.1 = (bf16[48,2304]{1,0:T(8,128)(2,1)}, bf16[48,2304]{1,0:T(8,128)(2,1)}, bf16[48,2304]{1,0:T(8,128)(2,1)}) custom-call(bf16[384,512]{1,0:T(8,128)(2,1)} %q_hbm.1, bf16[384,512]{1,0:T(8,128)(2,1)} %k_hbm.1, bf16[384,512]{1,0:T(8,128)(2,1)} %v_hbm.1, f32[384,512]{1,0:T(8,128)} %ld_hbm.1, f32[4,384]{1,0:T(4,128)} %bitcast.4, ...), custom_call_target="tpu_custom_call" | custom-call | tf_op jit(solution)/shard_map/delta_layer/pallas_call | solution.py:466
  41.1 1.9 %add_convert_fusion = bf16[48,2304]{1,0:T(8,128)(2,1)} fusion(bf16[48,2304]{1,0:T(8,128)(2,1)} %get-tuple-element.10, bf16[48,2304]{1,0:T(8,128)(2,1)} %get-tuple-element.9, bf16[48,2304]{1,0:T(8,128)(2,1)} %get-tuple-element.8), kind=kLoop, calls=%fused_computation | loop fusion | flops 663552 | bytes 884736 | tf_op jit(solution)/shard_map/convert_element_type | solution.py:520

commit v6 on v5

--- a/solution.py
+++ b/solution.py
@@ -64,6 +64,25 @@
     size = 1
     while size < W:
         mask = ((i // size) % 2 == 1) & ((j // size) == (i // size) - 1)
+        odd = range(size, W, 2 * size)
+        if size >= 16:
+            pick = jnp.concatenate([mask[lo : lo + size] for lo in odd], 0)
+            for b in blocks:
+                step = jnp.concatenate([b["a"][lo : lo + size] for lo in odd], 0)
+                st = mm(jnp.where(pick, step, zero[: W // 2]), b["t"]).astype(bf16)
+                full = []
+                for n in range(len(odd)):
+                    full += [zero[:size], st[n * size : (n + 1) * size]]
+                b["st"] = jnp.concatenate(full, 0)
+            for b in blocks:
+                rows = jnp.concatenate([b["t"][lo : lo + size] for lo in odd], 0)
+                rows = rows - mm(rows, b["st"])
+                full = []
+                for n, lo in enumerate(odd):
+                    full += [b["t"][lo - size : lo], rows[n * size : (n + 1) * size]]
+                b["t"] = jnp.concatenate(full, 0)
+            size *= 2
+            continue
         for b in blocks:
             step = jnp.where(mask, b["a"], zero)
             b["st"] = step if size == 1 else mm(step, b["t"]).astype(bf16)
@@ -188,9 +207,6 @@
     barrier = pltpu.get_barrier_semaphore()
     peers = [zdev(lax.rem(z + s, NZ)) for s in range(1, NZ)] + [ynext, yprev, sib]
     peers += [xdev(lax.rem(x + s, NX)) for s in range(1, NX)]
-    for peer in peers:
-        pl.semaphore_signal(barrier, inc=1, device_id=peer, device_id_type=MESH)
-
     loads = []
     for n, (src, dst) in enumerate(
         (
@@ -204,10 +220,12 @@
         )
     ):
         cp = pltpu.make_async_copy(src, dst, in_sem.at[n])
-        cp.start()
         loads.append(cp)
+        if n < 5:
+            cp.start()
     wown = pltpu.make_async_copy(w_hbm, weights.at[core], w_sem)
-    wown.start()
+    for peer in peers:
+        pl.semaphore_signal(barrier, inc=1, device_id=peer, device_id_type=MESH)
 
     def remote(src, dst, send, recv, dev):
         return pltpu.make_async_remote_copy(
@@ -256,6 +274,9 @@
 
     wsib = remote(w_hbm, weights.at[core], w_send, w_recv, sib)
     wsib.start()
+    for cp in loads[5:]:
+        cp.start()
+    wown.start()
 
     owner = z % 2 == core
     slot = (z // 4) + 2 * ((z // 2) % 2)
@@ -460,13 +481,13 @@
     kd, width = w.shape
     rb = toks // (NY * NC)
     tile = width // NT_OUT
-    anyspec = pl.BlockSpec(memory_space=pl.ANY)
+    anyspec = pl.BlockSpec(memory_space=pltpu.HBM)
     vmem, dma = pltpu.VMEM, pltpu.SemaphoreType.DMA
     out = jax.ShapeDtypeStruct((rb, width), bf16)
     own, one, two = pl.pallas_call(
         kernel,
         in_specs=[anyspec] * 8,
-        out_specs=[anyspec] * 3,
+        out_specs=[pl.BlockSpec(memory_space=pltpu.VMEM)] * 3,
         out_shape=[out] * 3,
         scratch_shapes=[
             vmem((toks, feats), bf16),
@@ -513,10 +534,10 @@
             dma((NT_OUT,)),
         ],
         compiler_params=pltpu.CompilerParams(
-            collective_id=0, has_side_effects=True, vmem_limit_bytes=56 << 20
+            collective_id=0, has_side_effects=True, vmem_limit_bytes=40 << 20
         ),
         name="delta_layer",
-    )(q, k, v, ld, wr.T, gate.reshape(NY, NC, rb, feats), gain.reshape(1, HS), w)
+    )(*[pltpu.with_memory_space_constraint(a, pltpu.HBM) for a in (q, k, v, ld, wr.T, gate.reshape(NY, NC, rb, feats), gain.reshape(1, HS), w)])
     return (own.astype(f32) + one.astype(f32) + two.astype(f32)).astype(bf16)
 
 

time: 43.1 us -> 41.8 us (0.970)
  other arithmetic: 1.92 us -> 0.77 us
    convert_element_type x1, other arithmetic: 1.92 us -> 0.77 us  [on_device(): return (own.astype(f32) + one.astype(f32) + two.astype(f32)).astype(bf16)]
where the time goes in v6:
time: 41.8 us; the launch traced here: 41.6 us
  Pallas kernels  40.8 us (98%)
  other arithmetic  0.77 us (2%)
    pallas_call x1, Pallas kernels, on_device(): pl.pallas_call(kernel, in_specs=[anyspec] * 8, out_specs=[pl.BlockSpec(me...  40.8 us

profile of v6, /device:TPU:6, one launch (start us, length us, event | category | flops | bytes accessed | tf_op | source)
XLA Modules:
  0.0 41.6 jit_solution(11256656106828378543)
XLA Ops:
  0.0 40.8 %delta_layer.1 = (bf16[48,2304]{1,0:T(8,128)(2,1)S(1)}, bf16[48,2304]{1,0:T(8,128)(2,1)S(1)}, bf16[48,2304]{1,0:T(8,128)(2,1)S(1)}) custom-call(bf16[384,512]{1,0:T(8,128)(2,1)} %q_hbm.1, bf16[384,512]{1,0:T(8,128)(2,1)} %k_hbm.1, bf16[384,512]{1,0:T(8,128)(2,1)} %v_hbm.1, f32[384,512]{1,0:T(8,128)} %ld_hbm.1, f32[4,384]{1,0:T(4,128)} %bitcast.4, ...), custom_call_target="tpu_custom_call" | custom-call | tf_op jit(solution)/shard_map/delta_layer/pallas_call | solution.py:487
  40.9 0.8 %add_convert_fusion = bf16[48,2304]{1,0:T(8,128)(2,1)} fusion(bf16[48,2304]{1,0:T(8,128)(2,1)S(1)} %get-tuple-element.10, bf16[48,2304]{1,0:T(8,128)(2,1)S(1)} %get-tuple-element.9, bf16[48,2304]{1,0:T(8,128)(2,1)S(1)} %get-tuple-element.8), kind=kLoop, calls=%fused_computation | loop fusion | flops 663552 | bytes 884736 | tf_op jit(solution)/shard_map/convert_element_type | solution.py:541

commit v7 on v6

--- a/solution.py
+++ b/solution.py
@@ -249,6 +249,8 @@
     cache = {}
     ti = lax.broadcasted_iota(jnp.int32, (MSG - 2 * HS, HS), 0)
     blocks, ends = prep_maps(heads, q_ref.shape[0] // W, read)
+    pl.semaphore_wait(barrier, len(peers))
+    sends = []
     for h, (take, state, total) in enumerate(ends):
         t1 = total.astype(bf16).astype(f32)
         t2 = (total - t1).astype(bf16).astype(f32)
@@ -257,11 +259,6 @@
         msg_ref[h, :HS] = take.astype(bf16)
         msg_ref[h, HS : 2 * HS] = state.astype(bf16)
         msg_ref[h, 2 * HS :] = tail.astype(bf16)
-
-    pl.semaphore_wait(barrier, len(peers))
-
-    sends = []
-    for h in range(heads):
         sends.append(remote(msg_ref.at[h], rmsg.at[z], m_send.at[h], m_recv.at[z], zdev(OWNER[h] + core)))
 
         @pl.when(z != OWNER[h] + core)
@@ -273,10 +270,8 @@
             rmsg[z] = msg_ref[h]
 
     wsib = remote(w_hbm, weights.at[core], w_send, w_recv, sib)
-    wsib.start()
     for cp in loads[5:]:
         cp.start()
-    wown.start()
 
     owner = z % 2 == core
     slot = (z // 4) + 2 * ((z // 2) % 2)
@@ -293,6 +288,8 @@
             lo = hi
 
     prep_reads(blocks, read, write)
+    wsib.start()
+    wown.start()
     for n in (5, 6):
         loads[n].wait()
     states = [remote(s_out, s_in, x_send.at[xx - 1], x_recv.at[0], xdev(xx)) for xx in (3, 2, 1)]

time: 41.8 us -> 41.7 us (level)
  no operation moved by 1% of the time
where the time goes in v7:
time: 41.7 us; the launch traced here: 41.6 us
  Pallas kernels  40.9 us (98%)
  other arithmetic  0.77 us (2%)
    pallas_call x1, Pallas kernels, on_device(): pl.pallas_call(kernel, in_specs=[anyspec] * 8, out_specs=[pl.BlockSpec(me...  40.9 us

profile of v7, /device:TPU:6, one launch (start us, length us, event | category | flops | bytes accessed | tf_op | source)
XLA Modules:
  0.0 41.6 jit_solution(4361049917672259067)
XLA Ops:
  0.0 40.9 %delta_layer.1 = (bf16[48,2304]{1,0:T(8,128)(2,1)S(1)}, bf16[48,2304]{1,0:T(8,128)(2,1)S(1)}, bf16[48,2304]{1,0:T(8,128)(2,1)S(1)}) custom-call(bf16[384,512]{1,0:T(8,128)(2,1)} %q_hbm.1, bf16[384,512]{1,0:T(8,128)(2,1)} %k_hbm.1, bf16[384,512]{1,0:T(8,128)(2,1)} %v_hbm.1, f32[384,512]{1,0:T(8,128)} %ld_hbm.1, f32[4,384]{1,0:T(4,128)} %bitcast.4, ...), custom_call_target="tpu_custom_call" | custom-call | tf_op jit(solution)/shard_map/delta_layer/pallas_call | solution.py:484
  40.9 0.8 %add_convert_fusion = bf16[48,2304]{1,0:T(8,128)(2,1)} fusion(bf16[48,2304]{1,0:T(8,128)(2,1)S(1)} %get-tuple-element.10, bf16[48,2304]{1,0:T(8,128)(2,1)S(1)} %get-tuple-element.9, bf16[48,2304]{1,0:T(8,128)(2,1)S(1)} %get-tuple-element.8), kind=kLoop, calls=%fused_computation | loop fusion | flops 663552 | bytes 884736 | tf_op jit(solution)/shard_map/convert_element_type | solution.py:538

commit v8 on v6

--- a/solution.py
+++ b/solution.py
@@ -163,7 +163,10 @@
     sin_out,
     sin,
     gated,
-    gsib,
+    qd_sib,
+    loc_sib,
+    gate_sib,
+    sin_sib,
     weights,
     acc,
     psend,
@@ -175,6 +178,8 @@
     x_recv,
     s_send,
     s_recv,
+    l_send,
+    l_recv,
     g_send,
     g_recv,
     w_sem,
@@ -273,7 +278,6 @@
             rmsg[z] = msg_ref[h]
 
     wsib = remote(w_hbm, weights.at[core], w_send, w_recv, sib)
-    wsib.start()
     for cp in loads[5:]:
         cp.start()
     wown.start()
@@ -293,6 +297,14 @@
             lo = hi
 
     prep_reads(blocks, read, write)
+    lent = [
+        remote(qd_ref.at[1 - core], qd_sib, l_send.at[0], l_recv.at[0], sib),
+        remote(loc_ref.at[1 - core], loc_sib, l_send.at[1], l_recv.at[1], sib),
+        remote(gate_hbm.at[:, 1 - core], gate_sib, l_send.at[2], l_recv.at[2], sib),
+    ]
+    for cp in lent:
+        cp.start()
+    wsib.start()
     for n in (5, 6):
         loads[n].wait()
     states = [remote(s_out, s_in, x_send.at[xx - 1], x_recv.at[0], xdev(xx)) for xx in (3, 2, 1)]
@@ -360,42 +372,41 @@
             cp.start()
         sin[slot] = sin_out[z]
 
-    def read(part, h):
+    def gate_of(att, gate):
+        ms = jnp.mean(att * att, axis=-1, keepdims=True)
+        gate = jax.nn.sigmoid(gate.astype(f32).reshape(NY * rows, HS))
+        return (att * lax.rsqrt(ms + 1e-5) * gain_ref[...] * gate).astype(bf16)
+
+    passed = []
+    for h in range(heads):
+
+        @pl.when(z != OWNER[h] + core)
+        def _(h=h):
+            remote(sin_out.at[0], sin.at[h], s_send.at[0], s_recv.at[h], zdev(OWNER[h] + core)).wait_recv()
+
+        cp = remote(sin.at[h], sin_sib.at[h], g_send.at[h], g_recv.at[h], sib)
+        cp.start()
+        passed.append(cp)
+    for h in range(heads):
         cols = slice(h * HS, (h + 1) * HS)
-        att = mm(qd_ref[part, :, cols], sin[h], NT) + loc_ref[part, :, cols]
-        ms = jnp.mean(att * att, axis=-1, keepdims=True)
-        gate = jax.nn.sigmoid(gate_ref[:, part, :, cols].astype(f32).reshape(NY * rows, HS))
-        return (att * lax.rsqrt(ms + 1e-5) * gain_ref[...] * gate).astype(bf16)
-
-    gcopies = []
-    for pair in range(heads // 2):
-        two = (2 * pair, 2 * pair + 1)
-        for h in two:
-
-            @pl.when(z != OWNER[h] + core)
-            def _(h=h):
-                remote(sin_out.at[0], sin.at[h], s_send.at[0], s_recv.at[h], zdev(OWNER[h] + core)).wait_recv()
-
-        out = [read(1 - core, h) for h in two]
-        cols = slice(two[0] * HS, (two[1] + 1) * HS)
-        gated[1 - core, :, cols] = jnp.concatenate(out, 1)
-        cp = remote(gated.at[1 - core, :, cols], gsib.at[:, cols], g_send.at[pair], g_recv.at[pair], sib)
-        cp.start()
-        gcopies.append(cp)
-    for h in range(heads):
-        gated[core, :, h * HS : (h + 1) * HS] = read(core, h)
+        att = mm(qd_ref[core, :, cols], sin[h], NT) + loc_ref[core, :, cols]
+        gated[0, :, cols] = gate_of(att, gate_ref[:, core, :, cols])
 
     started = []
     tile = weights.shape[2] // NT_OUT
     wide = 2 * tile
     wown.wait()
-    mine = gated[core]
+    mine = gated[0]
     for t in range(NT_OUT // 2):
         acc[t] = mm(mine, weights[core, :, t * wide : (t + 1) * wide])
+    for cp in lent + passed:
+        cp.wait()
+    for h in range(heads):
+        cols = slice(h * HS, (h + 1) * HS)
+        att = mm(qd_sib[:, cols], sin_sib[h], NT) + loc_sib[:, cols]
+        gated[1, :, cols] = gate_of(att, gate_sib[:, :, cols])
     wsib.wait()
-    for cp in gcopies:
-        cp.wait()
-    other = gsib[...]
+    other = gated[1]
     y1, y2, y3 = [lax.rem(y + s, NY) for s in range(1, NY)]
     for t in range(NT_OUT // 2):
         val = acc[t] + mm(other, weights[1 - core, :, t * wide : (t + 1) * wide])
@@ -512,6 +523,9 @@
             vmem((heads, HS, HS), bf16),
             vmem((NC, NY * rb, kd), bf16),
             vmem((NY * rb, kd), bf16),
+            vmem((NY * rb, kd), f32),
+            vmem((NY, rb, kd), bf16),
+            vmem((heads, HS, HS), bf16),
             vmem((NC, kd, width), bf16),
             vmem((NT_OUT // 2, NY * rb, 2 * tile), f32),
             vmem((NT_OUT, NY, rb, tile), bf16),
@@ -523,6 +537,8 @@
             dma((3,)),
             dma((NZ,)),
             dma((heads,)),
+            dma((3,)),
+            dma((3,)),
             dma((heads,)),
             dma((heads,)),
             dma,

time: 41.8 us -> 41.8 us (level)
  no operation moved by 1% of the time
where the time goes in v8:
time: 41.8 us; the launch traced here: 41.7 us
  Pallas kernels  40.9 us (98%)
  other arithmetic  0.77 us (2%)
    pallas_call x1, Pallas kernels, on_device(): pl.pallas_call(kernel, in_specs=[anyspec] * 8, out_specs=[pl.BlockSpec(me...  40.9 us

profile of v8, /device:TPU:6, one launch (start us, length us, event | category | flops | bytes accessed | tf_op | source)
XLA Modules:
  0.0 41.7 jit_solution(7921174516758739212)
XLA Ops:
  0.0 40.9 %delta_layer.1 = (bf16[48,2304]{1,0:T(8,128)(2,1)S(1)}, bf16[48,2304]{1,0:T(8,128)(2,1)S(1)}, bf16[48,2304]{1,0:T(8,128)(2,1)S(1)}) custom-call(bf16[384,512]{1,0:T(8,128)(2,1)} %q_hbm.1, bf16[384,512]{1,0:T(8,128)(2,1)} %k_hbm.1, bf16[384,512]{1,0:T(8,128)(2,1)} %v_hbm.1, f32[384,512]{1,0:T(8,128)} %ld_hbm.1, f32[4,384]{1,0:T(4,128)} %bitcast.4, ...), custom_call_target="tpu_custom_call" | custom-call | tf_op jit(solution)/shard_map/delta_layer/pallas_call | solution.py:498
  40.9 0.8 %add_convert_fusion = bf16[48,2304]{1,0:T(8,128)(2,1)} fusion(bf16[48,2304]{1,0:T(8,128)(2,1)S(1)} %get-tuple-element.10, bf16[48,2304]{1,0:T(8,128)(2,1)S(1)} %get-tuple-element.9, bf16[48,2304]{1,0:T(8,128)(2,1)S(1)} %get-tuple-element.8), kind=kLoop, calls=%fused_computation | loop fusion | flops 663552 | bytes 884736 | tf_op jit(solution)/shard_map/convert_element_type | solution.py:557
